TPU v7x, 32 devices: a whole 2x2x4 slice. The times are simulated.
32 devices in a mesh: chan: 4 (over x, core), rad: 8 (over z, y).
Axes of the slice: x: 2, y: 2, z: 4, core: 2. Of those that a mesh axis runs over, the one named last changes fastest.
Arguments:
- psi: float32 [2, 768, 128, 128], P(None, 'chan', 'rad'), may hold values from -6 to 6
- k_prev: float32 [2, 768, 128, 128], P(None, 'chan', 'rad'), may hold values from -6 to 6
- gaunt: bfloat16 [4, 768, 768], replicated, may hold values from -0.875 to 0.875
- dipole: bfloat16 [768, 768], replicated, may hold values from -0.875 to 0.875
- kinetic: float32 [128, 128], replicated, as said below
- chan_l: int32 [768, 2], P('chan'), may hold values from 0 to 23
- field_amp: float32 [1], replicated, may hold values from 0.02 to 0.1
Outputs:
- deriv: float32 [2, 768, 128, 128], P(None, 'chan', 'rad')
Inputs may be any that keep to these rules, and one draw needn't show every extreme that they name: `kinetic`: symmetric; zero where the row's and the column's blocks of 16 indices are more than one block apart.
All inputs are finite; a program needn't handle non-finite values.
Results may differ from a plain program's by a relative error of at most 0.00037.
Values may be sent and summed in bfloat16 or wider, within the bound.
A program may use at most 64 MiB of HBM per device.

v0:
```python
import functools

import jax
import jax.numpy as jnp
from jax import lax
from jax.experimental import pallas as pl
from jax.experimental.pallas import tpu as pltpu
from jax.sharding import PartitionSpec as P


def extended(array, sides, width):
    for axis, dim in sides:
        peers, length = (lax.axis_size(axis), array.shape[dim])
        up = [(i, (i + 1) % peers) for i in range(peers - 1)]
        down = [(j, i) for i, j in up]
        last = lax.slice_in_dim(array, length - width, length, axis=dim)
        initial = lax.slice_in_dim(array, 0, width, axis=dim)
        before = lax.ppermute(last, axis, up)
        after = lax.ppermute(initial, axis, down)
        array = jnp.concatenate([before, array, after], axis=dim)
    return array


def on_device(psi, k_prev, gaunt, dipole, kinetic, chan_l, field_amp):
    highest = lax.Precision.HIGHEST
    section = psi + 0.5 * k_prev
    local_chan = section.shape[1]
    rows = section.shape[2]
    width = section.shape[3]
    rad_at = lax.axis_index("rad")
    first_r = (
        1.0 + 8.0 * (rad_at * rows + jnp.arange(rows, dtype=jnp.int32)).astype(jnp.float32) / width
    )
    second_r = 1.0 + 8.0 * jnp.arange(width, dtype=jnp.float32) / width
    along_r2 = jnp.einsum("acij,kj->acik", section, kinetic, precision=highest)
    padded = extended(section.astype(jnp.bfloat16), (("rad", 2),), rows).astype(section.dtype)
    band = lax.dynamic_slice_in_dim(kinetic, rad_at * rows, rows, 0)
    widened = jnp.pad(band, ((0, 0), (rows, rows)))
    local_band = lax.dynamic_slice_in_dim(widened, rad_at * rows, 3 * rows, 1)
    along_r1 = jnp.einsum("ij,acjk->acik", local_band, padded, precision=highest)
    lvals = chan_l.astype(jnp.float32)
    first_l = lvals[:, 0] * (lvals[:, 0] + 1.0)
    second_l = lvals[:, 1] * (lvals[:, 1] + 1.0)
    potential = (
        first_l[:, None, None] / (2.0 * first_r * first_r)[None, :, None]
        + second_l[:, None, None] / (2.0 * second_r * second_r)[None, None, :]
        - 2.0 / first_r[None, :, None]
        - 2.0 / second_r[None, None, :]
    )
    sent = section.astype(jnp.bfloat16).reshape(2, local_chan, rows * width)
    chan_at = lax.axis_index("chan")
    block = lax.all_to_all(sent, "chan", split_axis=2, concat_axis=1, tiled=True)
    count = block.shape[2]
    place = chan_at * count + jnp.arange(count, dtype=jnp.int32)
    row_r = 1.0 + 8.0 * (rad_at * rows + place // width).astype(jnp.float32) / width
    col_r = 1.0 + 8.0 * (place % width).astype(jnp.float32) / width
    far = jnp.maximum(row_r, col_r)
    near = jnp.minimum(row_r, col_r)
    inverse = 1.0 / far
    ratio = near * inverse
    power = inverse
    total = jnp.zeros(block.shape, jnp.float32)
    for order in range(gaunt.shape[0]):
        mixed = jnp.einsum("cd,adq->acq", gaunt[order], block, preferred_element_type=jnp.float32)
        total = total + power[None, None, :] * mixed
        power = power * ratio
    mixed = jnp.einsum("cd,adq->acq", dipole, block, preferred_element_type=jnp.float32)
    total = total + (field_amp[0] * (row_r + col_r))[None, None, :] * mixed
    coupled = lax.all_to_all(
        total.astype(jnp.bfloat16), "chan", split_axis=1, concat_axis=2, tiled=True
    )
    coupled = coupled.reshape(coupled.shape[0], local_chan, rows, width)
    ham = along_r1 + along_r2 + potential[None] * section + coupled.astype(jnp.float32)
    return jnp.stack([ham[1], -ham[0]])


MESH = pl.DeviceIdType.MESH
GROUP = 16


def split_bf16(value):
    high = value.astype(jnp.bfloat16)
    return high, (value - high.astype(jnp.float32)).astype(jnp.bfloat16)


def fused_kernel(
    peers,
    rads,
    psi,
    k_prev,
    gaunt,
    dipole,
    kin_main,
    chan_main,
    field,
    out,
    kin,
    chan_l,
    pbuf,
    kbuf,
    sec,
    xg,
    halo,
    acc,
    acc1,
    weights,
    wr1,
    kk,
    lmul,
    langle,
    load_sem,
    weight_sem,
    hs,
    hr,
    xs,
    xr,
    cs,
    cr,
    fs,
    fr,
    ys,
    yr,
    zs,
    zr,
    small_sem,
):
    rows, chans, lanes = sec.shape
    width = lanes // 2
    orders = weights.shape[0]
    chips = peers // 2
    groups = chans // GROUP
    lead = rows // 4
    chan_at = lax.axis_index("chan")
    rad_at = lax.axis_index("rad")
    core = chan_at % 2
    chip = chan_at // 2
    partner = chan_at + 1 - 2 * core
    minor = rad_at % 2
    other = rad_at + 1 - 2 * minor
    ahead = rad_at + 2 - 4 * minor
    behind = rad_at - 2 + 4 * minor
    has_ahead = jnp.logical_and(ahead >= 0, ahead < rads)
    has_behind = jnp.logical_and(behind >= 0, behind < rads)
    near_slot = 1 - minor
    far_slot = minor

    def block(owner):
        return pl.ds(pl.multiple_of(owner * chans, GROUP), chans)

    def cut_of(group):
        return pl.ds(pl.multiple_of(group * GROUP, GROUP), GROUP)

    def block_cut(owner, group):
        return pl.ds(pl.multiple_of(owner * chans + group * GROUP, GROUP), GROUP)

    def chip_peer(step):
        return lax.rem(chip + step, chips) * 2 + core

    def chip_source(step):
        return lax.rem(chip - step + chips, chips) * 2 + core

    def load(which, group):
        source, target = ((psi, pbuf), (k_prev, kbuf))[which]
        return pltpu.make_async_copy(
            source.at[:, cut_of(group), :, :],
            target.at[:, cut_of(group), :, :],
            load_sem.at[which, group],
        )

    def load_weight(order):
        source = gaunt.at[order] if order < orders - 1 else dipole
        return pltpu.make_async_copy(
            source.at[block(chan_at), :], weights.at[order], weight_sem.at[order]
        )

    def remote(source, target, send, recv, device):
        return pltpu.make_async_remote_copy(
            src_ref=source,
            dst_ref=target,
            send_sem=send,
            recv_sem=recv,
            device_id=device,
            device_id_type=MESH,
        )

    def lead_copy(step, group, owner):
        view = xg.at[0:lead, block_cut(owner, group), :]
        device = {"chan": chip_peer(step)}
        return remote(view, view, hs.at[step - 1, group], hr.at[step - 1, group], device)

    def chip_copy(step, row, owner):
        view = xg.at[row, block(owner), :]
        device = {"chan": chip_peer(step)}
        return remote(view, view, xs.at[step - 1, row], xr.at[step - 1, row], device)

    def core_copy(index, owner):
        view = xg.at[index * lead : (index + 1) * lead, block(owner), :]
        return remote(view, view, cs.at[index], cr.at[index], {"chan": partner})

    def relay_lead(step, owner):
        view = xg.at[0:lead, block(owner), :]
        return remote(view, view, fs.at[step - 1, 0], fr.at[step - 1, 0], {"chan": partner})

    def relay_copy(step, row, owner):
        view = xg.at[row, block(owner), :]
        return remote(view, view, fs.at[step - 1, row], fr.at[step - 1, row], {"chan": partner})

    def half_of(half):
        return slice(half * (rows // 2), (half + 1) * (rows // 2))

    def side_copy(group, half):
        source = xg.at[half_of(half), block_cut(chan_at, group), :]
        target = halo.at[minor, half_of(half), cut_of(group), :]
        return remote(source, target, ys.at[half, group], yr.at[half, group], {"rad": other})

    def far_copy(group, half):
        source = halo.at[near_slot, half_of(half), cut_of(group), :]
        target = halo.at[minor, half_of(half), cut_of(group), :]
        return remote(source, target, zs.at[half, group], zr.at[half, group], {"rad": ahead})

    small = [
        pltpu.make_async_copy(kin_main, kin, small_sem.at[0]),
        pltpu.make_async_copy(chan_main, chan_l, small_sem.at[1]),
    ]
    depth = groups
    for group in range(depth):
        for which in range(2):
            load(which, group).start()

    barrier = pltpu.get_barrier_semaphore()
    for step in range(1, chips):
        pl.semaphore_signal(
            barrier, inc=1, device_id={"chan": chip_peer(step)}, device_id_type=MESH
        )
    pl.semaphore_signal(barrier, inc=1, device_id={"chan": partner}, device_id_type=MESH)
    pl.semaphore_signal(barrier, inc=1, device_id={"rad": other}, device_id_type=MESH)

    @pl.when(has_ahead)
    def _():
        pl.semaphore_signal(barrier, inc=1, device_id={"rad": ahead}, device_id_type=MESH)

    @pl.when(has_behind)
    def _():
        pl.semaphore_signal(barrier, inc=1, device_id={"rad": behind}, device_id_type=MESH)

    def form(group):
        for which in range(2):
            load(which, group).wait()

        for part in range(2):
            first = pbuf.at[part].reshape(chans * rows, width)
            second = kbuf.at[part].reshape(chans * rows, width)
            cut = slice(part * width, (part + 1) * width)
            for row in range(rows):
                place = (pl.ds(group * GROUP * rows + row, GROUP, stride=rows), slice(None))
                value = first[place] + 0.5 * second[place]
                sec[row, cut_of(group), cut] = value
                xg[row, block_cut(chan_at, group), cut] = value.astype(jnp.bfloat16)

    def send_group(group):
        for half in range(2):
            side_copy(group, half).start()
        for step in range(1, chips):
            lead_copy(step, group, chan_at).start()

    form(jnp.int32(0))
    pl.semaphore_wait(
        barrier, chips + 1 + has_ahead.astype(jnp.int32) + has_behind.astype(jnp.int32)
    )

    def form_next(group, carry):
        form(group)
        send_group(group - 1)
        return carry

    lax.fori_loop(1, groups, form_next, 0)
    for copy in small:
        copy.start()
    for order in range(orders):
        load_weight(order).start()

    send_group(groups - 1)
    for row in range(lead, rows):
        for step in range(1, chips):
            chip_copy(step, row, chan_at).start()
    for index in range(4):
        core_copy(index, chan_at).start()

    for copy in small:
        copy.wait()
    kin_high, kin_low = split_bf16(kin[...])
    both = jnp.concatenate([kin_high, kin_low], axis=1)
    kk[0:width, :] = both
    kk[width : 2 * width, :] = both

    band = kin[pl.ds(pl.multiple_of(rad_at * rows, rows), rows), :]
    size = rows * GROUP
    tall = jnp.broadcast_to(band[:, None, :], (rows, GROUP, width)).reshape(size, width)
    tall_high, tall_low = split_bf16(tall)
    at_row = lax.broadcasted_iota(jnp.int32, (size, size), 0)
    at_col = lax.broadcasted_iota(jnp.int32, (size, size), 1)
    same = (at_row % GROUP) == (at_col % GROUP)
    from_j = lax.broadcasted_iota(jnp.int32, (width, size), 0)
    to_col = lax.broadcasted_iota(jnp.int32, (width, size), 1)
    for side in range(3):
        pick = from_j == (rad_at + side - 1) * rows + to_col // GROUP
        pick = jnp.where(pick, 1.0, 0.0).astype(jnp.bfloat16)
        for level, source in enumerate((tall_high, tall_low)):
            wide = jnp.dot(source, pick, preferred_element_type=jnp.float32)
            wr1[side, level * size : (level + 1) * size, :] = jnp.where(same, wide, 0.0).astype(
                jnp.bfloat16
            )

    @pl.when(jnp.logical_not(has_behind))
    def _():
        halo[far_slot] = jnp.zeros(halo.shape[1:], halo.dtype)

    second_r = 1.0 + 8.0 * (
        lax.broadcasted_iota(jnp.int32, (1, lanes), 1) % width
    ).astype(jnp.float32) / width
    inner_r = second_r[:, :width]
    lvals = chan_l[...].astype(jnp.float32).astype(jnp.bfloat16)
    first = lax.broadcasted_iota(jnp.int32, (2, lanes), 0)
    spread = first == lax.broadcasted_iota(jnp.int32, (2, lanes), 1) // width
    spread = jnp.where(spread, 1.0, 0.0).astype(jnp.bfloat16)
    lwide = lax.dot_general(
        lvals, spread, (((0,), (0,)), ((), ())), preferred_element_type=jnp.float32
    )
    lwide = lwide * (lwide + 1.0)
    lmul[...] = lwide[:, :width]
    langle[...] = lwide[:, width:] / (2.0 * inner_r * inner_r) - 2.0 / inner_r

    def radius(row):
        place = jnp.full((1, lanes), rad_at * rows + row, jnp.int32)
        return 1.0 + 8.0 * place.astype(jnp.float32) / width

    for order in range(orders):
        load_weight(order).wait()

    def local_row(row):
        first_r = radius(row)[:, :width]
        scale = 1.0 / (2.0 * first_r * first_r)
        shift = 2.0 / first_r
        potential = lmul[...] * scale + langle[...] - shift
        for part in range(2):
            cut = slice(part * width, (part + 1) * width)
            value = sec[row, :, cut]
            high = xg[row, block(chan_at), cut]
            low = (value - high.astype(jnp.float32)).astype(jnp.bfloat16)
            both = jnp.dot(
                jnp.concatenate([high, low], axis=1), kk[...], preferred_element_type=jnp.float32
            )
            acc[row, :, cut] = both[:, :width] + both[:, width:] + potential * value

    def mix(side, value):
        both = jnp.dot(wr1[side], value, preferred_element_type=jnp.float32)
        return both[:size] + both[size:]

    def own_group(index):
        first = pl.multiple_of(index * GROUP, GROUP)
        start = pl.multiple_of(chan_at * chans + first, GROUP)
        high = xg[:, pl.ds(start, GROUP), :].reshape(size, lanes)
        value = sec[:, pl.ds(first, GROUP), :].reshape(size, lanes)
        low = (value - high.astype(jnp.float32)).astype(jnp.bfloat16)
        total = mix(1, high) + jnp.dot(
            wr1[1, 0:size, :], low, preferred_element_type=jnp.float32
        )
        acc1[:, pl.ds(first, GROUP), :] = total.reshape(rows, GROUP, lanes)

    def side_group(index):
        first = pl.multiple_of(index * GROUP, GROUP)
        cut = pl.ds(first, GROUP)
        total = mix(0, halo[0, :, cut, :].reshape(size, lanes)) + mix(
            2, halo[1, :, cut, :].reshape(size, lanes)
        )
        acc1[:, cut, :] = acc1[:, cut, :] + total.reshape(rows, GROUP, lanes)

    def couple(row):
        first_r = radius(row)
        inverse = 1.0 / jnp.maximum(first_r, second_r)
        ratio = jnp.minimum(first_r, second_r) * inverse
        factors = [inverse]
        for _ in range(orders - 2):
            factors.append(factors[-1] * ratio)
        factors.append(field[0] * (first_r + second_r))
        step = chans // 2
        for first in range(0, chans, step):
            total = jnp.zeros((step, lanes), jnp.float32)
            for order in range(orders):
                total = total + factors[order] * jnp.dot(
                    weights[order, first : first + step, :],
                    xg[row],
                    preferred_element_type=jnp.float32,
                )
            acc[row, first : first + step, :] = acc[row, first : first + step, :] + total.astype(
                jnp.bfloat16
            ).astype(jnp.float32)

    def relay(row):
        for step in range(1, chips):
            chip_copy(step, row, chip_source(step)).wait_recv()
            relay_copy(step, row, chip_source(step)).start()

    def take_row(row):
        for step in range(1, chips):
            relay_copy(step, row, chip_source(step) + 1 - 2 * core).wait_recv()
        couple(row)

    def pass_side(group):
        for half in range(2):
            side_copy(group, half).wait_recv()

            @pl.when(has_ahead)
            def _():
                far_copy(group, half).start()

    def take_side(group):
        @pl.when(has_behind)
        def _():
            for half in range(2):
                far_copy(group, half).wait_recv()

        side_group(group)

    early = groups // 4

    def begin(index, carry):
        own_group(index)
        for place in range(4):
            local_row(index * 4 + place)
        pass_side(index)
        return carry

    lax.fori_loop(0, early, begin, 0)
    for step in range(1, chips):
        for group in range(groups):
            lead_copy(step, group, chip_source(step)).wait_recv()
        relay_lead(step, chip_source(step)).start()
    for index in range(4):
        core_copy(index, partner).wait_recv()
    for step in range(1, chips):
        relay_lead(step, chip_source(step) + 1 - 2 * core).wait_recv()

    def main(index, carry):
        @pl.when(index + early < groups)
        def _():
            own_group(index + early)

        @pl.when(jnp.logical_and(index >= lead, index < 2 * lead))
        def _():
            local_row(index + rows - 2 * lead)

        late = early + index - index // 4

        @pl.when(index % 4 != 3)
        def _():
            pass_side(late)

        relay(lead + index)

        @pl.when(index < lead)
        def _():
            couple(index)

        @pl.when(index % 4 != 3)
        def _():
            take_side(late - early)

        @pl.when(index >= 1)
        def _():
            take_row(lead + index - 1)

        return carry

    lax.fori_loop(0, rows - lead, main, 0)

    def merge(group, some_rows):
        cut = cut_of(group)
        first = out.at[0].reshape(chans * rows, width)
        second = out.at[1].reshape(chans * rows, width)
        for row in some_rows:
            value = acc[row, cut, :] + acc1[row, cut, :]
            place = (pl.ds(group * GROUP * rows + row, GROUP, stride=rows), slice(None))
            first[place] = value[:, width:]
            second[place] = -value[:, :width]

    def merge_most(group, carry):
        merge(group, range(rows - 1))
        return carry

    def merge_last(group, carry):
        merge(group, range(rows - 1, rows))
        return carry

    def merge_side(group, carry):
        take_side(group)
        merge(group, range(rows))
        return carry

    lax.fori_loop(0, groups - early, merge_most, 0)
    take_row(rows - 1)
    lax.fori_loop(0, groups - early, merge_last, 0)
    lax.fori_loop(groups - early, groups, merge_side, 0)

    def drain_row(row, carry):
        for step in range(1, chips):
            chip_copy(step, row, chan_at).wait_send()
            relay_copy(step, row, chip_source(step)).wait_send()
        return carry

    def drain_group(group, carry):
        for step in range(1, chips):
            lead_copy(step, group, chan_at).wait_send()
        for half in range(2):
            side_copy(group, half).wait_send()

        @pl.when(has_ahead)
        def _():
            for half in range(2):
                far_copy(group, half).wait_send()

        return carry

    for index in range(4):
        core_copy(index, chan_at).wait_send()
    for step in range(1, chips):
        relay_lead(step, chip_source(step)).wait_send()
    lax.fori_loop(lead, rows, drain_row, 0)
    lax.fori_loop(0, groups, drain_group, 0)


def device_step(peers, rads, psi, k_prev, gaunt, dipole, kinetic, chan_l, field_amp):
    _, chans, rows, width = psi.shape
    fits = (
        chans == 3 * 4 * GROUP
        and rows == GROUP
        and peers % 2 == 0
        and rads % 2 == 0
        and width == rads * rows
        and width == 128
    )
    if not fits:
        return on_device(psi, k_prev, gaunt, dipole, kinetic, chan_l, field_amp)
    orders = gaunt.shape[0] + 1
    chips = peers // 2
    groups = chans // GROUP
    lanes = 2 * width
    size = rows * GROUP
    f32, bf16, dma = (jnp.float32, jnp.bfloat16, pltpu.SemaphoreType.DMA)
    main_memory = pl.BlockSpec(memory_space=pltpu.HBM)
    vmem = pl.BlockSpec(memory_space=pltpu.VMEM)
    psi, k_prev, gaunt, dipole, kinetic, chan_l = (
        pltpu.with_memory_space_constraint(value, pltpu.HBM)
        for value in (psi, k_prev, gaunt, dipole, kinetic, chan_l.T)
    )
    return pl.pallas_call(
        functools.partial(fused_kernel, peers, rads),
        out_shape=jax.ShapeDtypeStruct(psi.shape, f32),
        in_specs=[main_memory] * 6 + [pl.BlockSpec(memory_space=pltpu.SMEM)],
        out_specs=vmem,
        scratch_shapes=[
            pltpu.VMEM(kinetic.shape, f32),
            pltpu.VMEM((2, chans), jnp.int32),
            pltpu.VMEM((2, chans, rows, width), f32),
            pltpu.VMEM((2, chans, rows, width), f32),
            pltpu.VMEM((rows, chans, lanes), f32),
            pltpu.VMEM((rows, peers * chans, lanes), bf16),
            pltpu.VMEM((2, rows, chans, lanes), bf16),
            pltpu.VMEM((rows, chans, lanes), f32),
            pltpu.VMEM((rows, chans, lanes), f32),
            pltpu.VMEM((orders, chans, peers * chans), bf16),
            pltpu.VMEM((3, 2 * size, size), bf16),
            pltpu.VMEM((lanes, lanes), bf16),
            pltpu.VMEM((chans, width), f32),
            pltpu.VMEM((chans, width), f32),
            dma((2, groups)),
            dma((orders,)),
            dma((chips - 1, groups)),
            dma((chips - 1, groups)),
            dma((chips - 1, rows)),
            dma((chips - 1, rows)),
            dma((4,)),
            dma((4,)),
            dma((chips - 1, rows)),
            dma((chips - 1, rows)),
            dma((2, groups)),
            dma((2, groups)),
            dma((2, groups)),
            dma((2, groups)),
            dma((2,)),
        ],
        compiler_params=pltpu.CompilerParams(
            collective_id=0, has_side_effects=True, vmem_limit_bytes=36 * 1024 * 1024
        ),
    )(psi, k_prev, gaunt, dipole, kinetic, chan_l, field_amp)


def solution(mesh):
    placed = (
        P(None, "chan", "rad", None),
        P(None, "chan", "rad", None),
        P(),
        P(),
        P(),
        P("chan", None),
        P(),
    )
    return jax.shard_map(
        functools.partial(device_step, mesh.shape["chan"], mesh.shape["rad"]),
        mesh=mesh,
        in_specs=placed,
        out_specs=P(None, "chan", "rad", None),
        check_vma=False,
    )
```

profile of v0, /device:TPU:0, one launch (start us, length us, event | category | flops | bytes accessed | tf_op | source)
XLA Modules:
  0.0 48.3 jit_solution(6105360961943990251)
XLA Ops:
  0.7 45.9 %shard_map.73 = f32[2,192,16,128]{3,2,1,0:T(8,128)S(1)} custom-call(f32[2,192,16,128]{3,2,1,0:T(8,128)} %psi.1, f32[2,192,16,128]{3,2,1,0:T(8,128)} %k_prev.1, bf16[4,768,768]{2,1,0:T(8,128)(2,1)} %gaunt.1, bf16[768,768]{1,0:T(8,128)(2,1)} %dipole.1, f32[128,128]{1,0:T(8,128)} %kin_main.1, s32[2,192]{1,0:T(2,128)} %bitcast.1, f32[1]{0:T(128)S(6)} %copy.9.field), custom_call_target="tpu_custom_call" | custom-call | tf_op jit(solution)/shard_map/pallas_call | solution.py:556
  46.6 1.7 %copy.10 = f32[2,192,16,128]{3,2,1,0:T(8,128)} copy(f32[2,192,16,128]{3,2,1,0:T(8,128)S(1)} %shard_map.73) | data formatting | bytes 6291456
where the time goes:
time: 48.5 us; the launch traced here: 48.3 us
  Pallas kernels  45.9 us (95%)
  local copies, waits for them, and re-layouts  1.67 us (3%)
  between operations  0.66 us (1%)
    pallas_call x1, Pallas kernels, device_step(): pl.pallas_call(functools.partial(fused_kernel, peers, rads), out_shape=ja...  45.9 us
    unnamed x1, local copies, waits for them, and re-layouts  1.67 us

commit v1 on v0

--- a/solution.py
+++ b/solution.py
@@ -76,6 +76,7 @@
 
 MESH = pl.DeviceIdType.MESH
 GROUP = 16
+LOADS = ((0, 1), (1, 2), (2, 4), (4, 8), (8, 12))
 
 
 def split_bf16(value):
@@ -109,7 +110,7 @@
     lmul,
     langle,
     load_sem,
-    weight_sem,
+    small_sem,
     hs,
     hr,
     xs,
@@ -117,12 +118,12 @@
     cs,
     cr,
     fs,
+    fl,
     fr,
     ys,
     yr,
     zs,
     zr,
-    small_sem,
 ):
     rows, chans, lanes = sec.shape
     width = lanes // 2
@@ -159,18 +160,18 @@
     def chip_source(step):
         return lax.rem(chip - step + chips, chips) * 2 + core
 
-    def load(which, group):
+    def load(which, part):
         source, target = ((psi, pbuf), (k_prev, kbuf))[which]
+        first, last = LOADS[part]
+        cut = slice(first * GROUP, last * GROUP)
         return pltpu.make_async_copy(
-            source.at[:, cut_of(group), :, :],
-            target.at[:, cut_of(group), :, :],
-            load_sem.at[which, group],
+            source.at[:, cut, :, :], target.at[:, cut, :, :], load_sem.at[which, part]
         )
 
     def load_weight(order):
         source = gaunt.at[order] if order < orders - 1 else dipole
         return pltpu.make_async_copy(
-            source.at[block(chan_at), :], weights.at[order], weight_sem.at[order]
+            source.at[block(chan_at), :], weights.at[order], small_sem.at[2]
         )
 
     def remote(source, target, send, recv, device):
@@ -183,27 +184,27 @@
             device_id_type=MESH,
         )
 
-    def lead_copy(step, group, owner):
-        view = xg.at[0:lead, block_cut(owner, group), :]
+    def lead_copy(step, some, owner):
+        view = xg.at[0:lead, some, :]
         device = {"chan": chip_peer(step)}
-        return remote(view, view, hs.at[step - 1, group], hr.at[step - 1, group], device)
-
-    def chip_copy(step, row, owner):
-        view = xg.at[row, block(owner), :]
+        return remote(view, view, hs.at[step - 1], hr.at[step - 1], device)
+
+    def chip_copy(step, some_rows, owner, place):
+        view = xg.at[some_rows, block(owner), :]
         device = {"chan": chip_peer(step)}
-        return remote(view, view, xs.at[step - 1, row], xr.at[step - 1, row], device)
-
-    def core_copy(index, owner):
-        view = xg.at[index * lead : (index + 1) * lead, block(owner), :]
-        return remote(view, view, cs.at[index], cr.at[index], {"chan": partner})
+        return remote(view, view, xs.at[step - 1], xr.at[step - 1, place], device)
+
+    def core_copy(some_rows, owner):
+        view = xg.at[some_rows, block(owner), :]
+        return remote(view, view, cs, cr, {"chan": partner})
 
     def relay_lead(step, owner):
         view = xg.at[0:lead, block(owner), :]
-        return remote(view, view, fs.at[step - 1, 0], fr.at[step - 1, 0], {"chan": partner})
-
-    def relay_copy(step, row, owner):
-        view = xg.at[row, block(owner), :]
-        return remote(view, view, fs.at[step - 1, row], fr.at[step - 1, row], {"chan": partner})
+        return remote(view, view, fs.at[step - 1], fl.at[step - 1], {"chan": partner})
+
+    def relay_copy(step, some_rows, owner, place):
+        view = xg.at[some_rows, block(owner), :]
+        return remote(view, view, fs.at[step - 1], fr.at[step - 1, place], {"chan": partner})
 
     def half_of(half):
         return slice(half * (rows // 2), (half + 1) * (rows // 2))
@@ -211,21 +212,21 @@
     def side_copy(group, half):
         source = xg.at[half_of(half), block_cut(chan_at, group), :]
         target = halo.at[minor, half_of(half), cut_of(group), :]
-        return remote(source, target, ys.at[half, group], yr.at[half, group], {"rad": other})
-
-    def far_copy(group, half):
-        source = halo.at[near_slot, half_of(half), cut_of(group), :]
-        target = halo.at[minor, half_of(half), cut_of(group), :]
-        return remote(source, target, zs.at[half, group], zr.at[half, group], {"rad": ahead})
-
+        return remote(source, target, ys, yr.at[half, group], {"rad": other})
+
+    def far_copy(some_rows, some, place):
+        source = halo.at[near_slot, some_rows, some, :]
+        target = halo.at[minor, some_rows, some, :]
+        return remote(source, target, zs, zr.at[place], {"rad": ahead})
+
+    every = slice(0, rows)
     small = [
         pltpu.make_async_copy(kin_main, kin, small_sem.at[0]),
         pltpu.make_async_copy(chan_main, chan_l, small_sem.at[1]),
     ]
-    depth = groups
-    for group in range(depth):
+    for part in range(len(LOADS)):
         for which in range(2):
-            load(which, group).start()
+            load(which, part).start()
 
     barrier = pltpu.get_barrier_semaphore()
     for step in range(1, chips):
@@ -244,9 +245,6 @@
         pl.semaphore_signal(barrier, inc=1, device_id={"rad": behind}, device_id_type=MESH)
 
     def form(group):
-        for which in range(2):
-            load(which, group).wait()
-
         for part in range(2):
             first = pbuf.at[part].reshape(chans * rows, width)
             second = kbuf.at[part].reshape(chans * rows, width)
@@ -261,19 +259,29 @@
         for half in range(2):
             side_copy(group, half).start()
         for step in range(1, chips):
-            lead_copy(step, group, chan_at).start()
-
+            lead_copy(step, block_cut(chan_at, group), chan_at).start()
+
+    def arrive(part):
+        for which in range(2):
+            load(which, part).wait()
+
+    arrive(0)
     form(jnp.int32(0))
     pl.semaphore_wait(
         barrier, chips + 1 + has_ahead.astype(jnp.int32) + has_behind.astype(jnp.int32)
     )
+    send_group(0)
+    arrive(1)
+    form(jnp.int32(1))
 
     def form_next(group, carry):
         form(group)
         send_group(group - 1)
         return carry
 
-    lax.fori_loop(1, groups, form_next, 0)
+    for part in range(2, len(LOADS)):
+        arrive(part)
+        lax.fori_loop(LOADS[part][0], LOADS[part][1], form_next, 0)
     for copy in small:
         copy.start()
     for order in range(orders):
@@ -282,10 +290,18 @@
     send_group(groups - 1)
     for row in range(lead, rows):
         for step in range(1, chips):
-            chip_copy(step, row, chan_at).start()
+            chip_copy(step, row, chan_at, row - lead).start()
     for index in range(4):
-        core_copy(index, chan_at).start()
-
+        core_copy(slice(index * lead, (index + 1) * lead), chan_at).start()
+
+    def forward(group, half):
+        side_copy(group, half).wait_recv()
+
+        @pl.when(has_ahead)
+        def _():
+            far_copy(half_of(half), cut_of(group), group).start()
+
+    forward(0, 0)
     for copy in small:
         copy.wait()
     kin_high, kin_low = split_bf16(kin[...])
@@ -333,9 +349,6 @@
     def radius(row):
         place = jnp.full((1, lanes), rad_at * rows + row, jnp.int32)
         return 1.0 + 8.0 * place.astype(jnp.float32) / width
-
-    for order in range(orders):
-        load_weight(order).wait()
 
     def local_row(row):
         first_r = radius(row)[:, :width]
@@ -398,81 +411,94 @@
 
     def relay(row):
         for step in range(1, chips):
-            chip_copy(step, row, chip_source(step)).wait_recv()
-            relay_copy(step, row, chip_source(step)).start()
+            chip_copy(step, row, chip_source(step), row - lead).wait_recv()
+            relay_copy(step, row, chip_source(step), row - lead).start()
 
     def take_row(row):
         for step in range(1, chips):
-            relay_copy(step, row, chip_source(step) + 1 - 2 * core).wait_recv()
+            owner = chip_source(step) + 1 - 2 * core
+            relay_copy(step, row, owner, row - lead).wait_recv()
         couple(row)
-
-    def pass_side(group):
-        for half in range(2):
-            side_copy(group, half).wait_recv()
-
-            @pl.when(has_ahead)
-            def _():
-                far_copy(group, half).start()
 
     def take_side(group):
         @pl.when(has_behind)
         def _():
-            for half in range(2):
-                far_copy(group, half).wait_recv()
+            far_copy(every, cut_of(group), group).wait_recv()
 
         side_group(group)
 
-    early = groups // 4
-
-    def begin(index, carry):
+    forward(0, 1)
+    for index in range(2):
         own_group(index)
-        for place in range(4):
-            local_row(index * 4 + place)
-        pass_side(index)
+    for index in range(3):
+        local_row(index)
+
+    def phase(index, carry):
+        for half in range(2):
+            forward(index + 1, half)
+            for place in range(2):
+                own_group(index * 4 + half * 2 + place + 2)
+            for place in range(3 - half):
+                local_row(index * 5 + half * 3 + place + 3)
         return carry
 
-    lax.fori_loop(0, early, begin, 0)
+    lax.fori_loop(0, 2, phase, 0)
     for step in range(1, chips):
-        for group in range(groups):
-            lead_copy(step, group, chip_source(step)).wait_recv()
+        lead_copy(step, block(chip_source(step)), chip_source(step)).wait_recv()
         relay_lead(step, chip_source(step)).start()
-    for index in range(4):
-        core_copy(index, partner).wait_recv()
-    for step in range(1, chips):
-        relay_lead(step, chip_source(step) + 1 - 2 * core).wait_recv()
+    pltpu.make_async_copy(weights, weights, small_sem.at[2]).wait()
+    core_copy(every, partner).wait_recv()
+    for index in range(2):
+        own_group(index + 10)
 
     def main(index, carry):
-        @pl.when(index + early < groups)
+        start = index * lead
+
+        def when_first(work, *args):
+            @pl.when(index == 1)
+            def _():
+                work(*args)
+
+        def lead_or_row(row):
+            @pl.when(index == 1)
+            def _():
+                couple(row)
+
+            @pl.when(index > 1)
+            def _():
+                take_row(row)
+
+        forward(3 * index, 0)
+
+        @pl.when(index == 1)
         def _():
-            own_group(index + early)
-
-        @pl.when(jnp.logical_and(index >= lead, index < 2 * lead))
-        def _():
-            local_row(index + rows - 2 * lead)
-
-        late = early + index - index // 4
-
-        @pl.when(index % 4 != 3)
-        def _():
-            pass_side(late)
-
-        relay(lead + index)
-
-        @pl.when(index < lead)
-        def _():
-            couple(index)
-
-        @pl.when(index % 4 != 3)
-        def _():
-            take_side(late - early)
-
-        @pl.when(index >= 1)
-        def _():
-            take_row(lead + index - 1)
-
+            for row in range(13, rows):
+                local_row(row)
+            for step in range(1, chips):
+                relay_lead(step, chip_source(step) + 1 - 2 * core).wait_recv()
+
+        lead_or_row(start - 2)
+        forward(3 * index, 1)
+        relay(start)
+        take_side(3 * index - 2)
+        lead_or_row(start - 1)
+        forward(3 * index + 1, 0)
+        relay(start + 1)
+        take_side(3 * index - 1)
+        when_first(take_side, 0)
+        when_first(couple, 0)
+        forward(3 * index + 1, 1)
+        take_row(start)
+        forward(3 * index + 2, 0)
+        relay(start + 2)
+        take_row(start + 1)
+        forward(3 * index + 2, 1)
+        relay(start + 3)
+        take_side(3 * index)
+        when_first(couple, 1)
         return carry
 
-    lax.fori_loop(0, rows - lead, main, 0)
+    lax.fori_loop(1, 4, main, 0)
 
     def merge(group, some_rows):
         cut = cut_of(group)
@@ -492,41 +518,25 @@
         merge(group, range(rows - 1, rows))
         return carry
 
-    def merge_side(group, carry):
-        take_side(group)
-        merge(group, range(rows))
-        return carry
-
-    lax.fori_loop(0, groups - early, merge_most, 0)
+    take_row(rows - 2)
+    lax.fori_loop(0, groups - 2, merge_most, 0)
+    take_side(groups - 2)
+    merge(groups - 2, range(rows - 1))
     take_row(rows - 1)
-    lax.fori_loop(0, groups - early, merge_last, 0)
-    lax.fori_loop(groups - early, groups, merge_side, 0)
-
-    def drain_row(row, carry):
-        for step in range(1, chips):
-            chip_copy(step, row, chan_at).wait_send()
-            relay_copy(step, row, chip_source(step)).wait_send()
-        return carry
-
-    def drain_group(group, carry):
-        for step in range(1, chips):
-            lead_copy(step, group, chan_at).wait_send()
-        for half in range(2):
-            side_copy(group, half).wait_send()
-
-        @pl.when(has_ahead)
-        def _():
-            for half in range(2):
-                far_copy(group, half).wait_send()
-
-        return carry
-
-    for index in range(4):
-        core_copy(index, chan_at).wait_send()
+    lax.fori_loop(0, groups - 1, merge_last, 0)
+    take_side(groups - 1)
+    merge(groups - 1, range(rows))
+
+    core_copy(every, chan_at).wait_send()
     for step in range(1, chips):
-        relay_lead(step, chip_source(step)).wait_send()
-    lax.fori_loop(lead, rows, drain_row, 0)
-    lax.fori_loop(0, groups, drain_group, 0)
+        lead_copy(step, block(chan_at), chan_at).wait_send()
+        chip_copy(step, slice(lead, rows), chan_at, 0).wait_send()
+        relay_copy(step, every, chip_source(step), 0).wait_send()
+    remote(xg.at[:, block(chan_at), :], halo.at[minor], ys, yr.at[0, 0], {"rad": other}).wait_send()
+
+    @pl.when(has_ahead)
+    def _():
+        far_copy(every, slice(0, chans), 0).wait_send()
 
 
 def device_step(peers, rads, psi, k_prev, gaunt, dipole, kinetic, chan_l, field_amp):
@@ -573,21 +583,21 @@
             pltpu.VMEM((lanes, lanes), bf16),
             pltpu.VMEM((chans, width), f32),
             pltpu.VMEM((chans, width), f32),
+            dma((2, len(LOADS))),
+            dma((3,)),
+            dma((chips - 1,)),
+            dma((chips - 1,)),
+            dma((chips - 1,)),
+            dma((chips - 1, rows - rows // 4)),
+            dma,
+            dma,
+            dma((chips - 1,)),
+            dma((chips - 1,)),
+            dma((chips - 1, rows - rows // 4)),
+            dma,
             dma((2, groups)),
-            dma((orders,)),
-            dma((chips - 1, groups)),
-            dma((chips - 1, groups)),
-            dma((chips - 1, rows)),
-            dma((chips - 1, rows)),
-            dma((4,)),
-            dma((4,)),
-            dma((chips - 1, rows)),
-            dma((chips - 1, rows)),
-            dma((2, groups)),
-            dma((2, groups)),
-            dma((2, groups)),
-            dma((2, groups)),
-            dma((2,)),
+            dma,
+            dma((groups,)),
         ],
         compiler_params=pltpu.CompilerParams(
             collective_id=0, has_side_effects=True, vmem_limit_bytes=36 * 1024 * 1024

time: 48.5 us -> 45.9 us (0.946)
  Pallas kernels: 45.9 us -> 43.4 us
    pallas_call x1, Pallas kernels: 45.9 us -> 43.4 us  [device_step(): pl.pallas_call(functools.partial(fused_kernel, peers, rads), out_shape=ja...]
where the time goes in v1:
time: 45.9 us; the launch traced here: 45.7 us
  Pallas kernels  43.4 us (95%)
  local copies, waits for them, and re-layouts  1.67 us (4%)
  between operations  0.66 us (1%)
    pallas_call x1, Pallas kernels, device_step(): pl.pallas_call(functools.partial(fused_kernel, peers, rads), out_shape=ja...  43.4 us
    unnamed x1, local copies, waits for them, and re-layouts  1.67 us

profile of v1, /device:TPU:0, one launch (start us, length us, event | category | flops | bytes accessed | tf_op | source)
XLA Modules:
  0.0 45.7 jit_solution(4853531680932728915)
XLA Ops:
  0.7 43.4 %shard_map.73 = f32[2,192,16,128]{3,2,1,0:T(8,128)S(1)} custom-call(f32[2,192,16,128]{3,2,1,0:T(8,128)} %psi.1, f32[2,192,16,128]{3,2,1,0:T(8,128)} %k_prev.1, bf16[4,768,768]{2,1,0:T(8,128)(2,1)} %gaunt.1, bf16[768,768]{1,0:T(8,128)(2,1)} %dipole.1, f32[128,128]{1,0:T(8,128)} %kin_main.1, s32[2,192]{1,0:T(2,128)} %bitcast.1, f32[1]{0:T(128)S(6)} %copy.9.field), custom_call_target="tpu_custom_call" | custom-call | tf_op jit(solution)/shard_map/pallas_call | solution.py:566
  44.1 1.7 %copy.10 = f32[2,192,16,128]{3,2,1,0:T(8,128)} copy(f32[2,192,16,128]{3,2,1,0:T(8,128)S(1)} %shard_map.73) | data formatting | bytes 6291456

commit v2 on v1

--- a/solution.py
+++ b/solution.py
@@ -97,14 +97,17 @@
     out,
     kin,
     chan_l,
-    pbuf,
-    kbuf,
+    pk,
     sec,
     xg,
+    xp,
+    coupled,
+    back,
     halo,
     acc,
     acc1,
     weights,
+    peer_weights,
     wr1,
     kk,
     lmul,
@@ -124,6 +127,9 @@
     yr,
     zs,
     zr,
+    vs,
+    vr,
+    via,
 ):
     rows, chans, lanes = sec.shape
     width = lanes // 2
@@ -144,6 +150,8 @@
     has_behind = jnp.logical_and(behind >= 0, behind < rads)
     near_slot = 1 - minor
     far_slot = minor
+    whole = rows - 2
+    peer = lax.rem(chip + 1, chips) * 2 + core
 
     def block(owner):
         return pl.ds(pl.multiple_of(owner * chans, GROUP), chans)
@@ -161,17 +169,27 @@
         return lax.rem(chip - step + chips, chips) * 2 + core
 
     def load(which, part):
-        source, target = ((psi, pbuf), (k_prev, kbuf))[which]
         first, last = LOADS[part]
         cut = slice(first * GROUP, last * GROUP)
         return pltpu.make_async_copy(
-            source.at[:, cut, :, :], target.at[:, cut, :, :], load_sem.at[which, part]
+            (psi, k_prev)[which].at[:, cut, :, :], pk.at[which, :, cut, :, :], load_sem.at[part]
         )
+
+    def arrive(part):
+        first, last = LOADS[part]
+        view = pk.at[:, :, first * GROUP : last * GROUP, :, :]
+        pltpu.make_async_copy(view, view, load_sem.at[part]).wait()
 
     def load_weight(order):
         source = gaunt.at[order] if order < orders - 1 else dipole
         return pltpu.make_async_copy(
             source.at[block(chan_at), :], weights.at[order], small_sem.at[2]
+        )
+
+    def load_peer_weight(order):
+        source = gaunt.at[order] if order < orders - 1 else dipole
+        return pltpu.make_async_copy(
+            source.at[block(peer), :], peer_weights.at[order], small_sem.at[3]
         )
 
     def remote(source, target, send, recv, device):
@@ -184,27 +202,44 @@
             device_id_type=MESH,
         )
 
-    def lead_copy(step, some, owner):
+    def lead_copy(some):
         view = xg.at[0:lead, some, :]
-        device = {"chan": chip_peer(step)}
-        return remote(view, view, hs.at[step - 1], hr.at[step - 1], device)
-
-    def chip_copy(step, some_rows, owner, place):
-        view = xg.at[some_rows, block(owner), :]
-        device = {"chan": chip_peer(step)}
-        return remote(view, view, xs.at[step - 1], xr.at[step - 1, place], device)
+        return remote(view, view, hs, hr, {"chan": peer})
+
+    def chip_copy(row, owner):
+        view = xg.at[row, block(owner), :]
+        return remote(view, view, xs, xr.at[row - lead], {"chan": peer})
+
+    def part_copy(part, owner):
+        view = xp.at[part, block(owner), :]
+        return remote(view, view, xs, xr.at[whole - lead], {"chan": peer})
+
+    def back_copy(part):
+        return remote(back, coupled.at[part], xs, xr.at[whole - lead + 1], {"chan": peer})
 
     def core_copy(some_rows, owner):
         view = xg.at[some_rows, block(owner), :]
-        return remote(view, view, cs, cr, {"chan": partner})
-
-    def relay_lead(step, owner):
+        return remote(view, view, cs, cr.at[0], {"chan": partner})
+
+    def core_part(owner):
+        view = xp.at[chip, block(owner), :]
+        return remote(view, view, cs, cr.at[1], {"chan": partner})
+
+    def relay_lead(owner):
         view = xg.at[0:lead, block(owner), :]
-        return remote(view, view, fs.at[step - 1], fl.at[step - 1], {"chan": partner})
-
-    def relay_copy(step, some_rows, owner, place):
-        view = xg.at[some_rows, block(owner), :]
-        return remote(view, view, fs.at[step - 1], fr.at[step - 1, place], {"chan": partner})
+        return remote(view, view, fs, fl, {"chan": partner})
+
+    def relay_copy(row, owner):
+        view = xg.at[row, block(owner), :]
+        return remote(view, view, fs, fr.at[row - lead], {"chan": partner})
+
+    def relay_part(owner):
+        view = xp.at[chip, block(owner), :]
+        return remote(view, view, fs, fr.at[whole - lead], {"chan": partner})
+
+    def sent(count, sem, device):
+        view = xg.at[0:count, block(chan_at), :]
+        remote(view, view, sem, fl, device).wait_send()
 
     def half_of(half):
         return slice(half * (rows // 2), (half + 1) * (rows // 2))
@@ -218,6 +253,14 @@
         source = halo.at[near_slot, some_rows, some, :]
         target = halo.at[minor, some_rows, some, :]
         return remote(source, target, zs, zr.at[place], {"rad": ahead})
+
+    def via_copy():
+        source = xg.at[half_of(1), block_cut(chan_at, groups - 1), :]
+        return remote(source, via, vs.at[0], vr.at[0], {"rad": behind})
+
+    def via_forward():
+        target = halo.at[near_slot, half_of(1), cut_of(groups - 1), :]
+        return remote(via, target, vs.at[1], vr.at[1], {"rad": other})
 
     every = slice(0, rows)
     small = [
@@ -246,24 +289,23 @@
 
     def form(group):
         for part in range(2):
-            first = pbuf.at[part].reshape(chans * rows, width)
-            second = kbuf.at[part].reshape(chans * rows, width)
+            first = pk.at[0, part].reshape(chans * rows, width)
+            second = pk.at[1, part].reshape(chans * rows, width)
             cut = slice(part * width, (part + 1) * width)
             for row in range(rows):
                 place = (pl.ds(group * GROUP * rows + row, GROUP, stride=rows), slice(None))
                 value = first[place] + 0.5 * second[place]
                 sec[row, cut_of(group), cut] = value
-                xg[row, block_cut(chan_at, group), cut] = value.astype(jnp.bfloat16)
+                rounded = value.astype(jnp.bfloat16)
+                xg[row, block_cut(chan_at, group), cut] = rounded
+                if row >= whole:
+                    lane = slice((row - whole) * width, (row - whole + 1) * width)
+                    xp[part, block_cut(chan_at, group), lane] = rounded
 
     def send_group(group):
         for half in range(2):
             side_copy(group, half).start()
-        for step in range(1, chips):
-            lead_copy(step, block_cut(chan_at, group), chan_at).start()
-
-    def arrive(part):
-        for which in range(2):
-            load(which, part).wait()
+        lead_copy(block_cut(chan_at, group)).start()
 
     arrive(0)
     form(jnp.int32(0))
@@ -286,13 +328,20 @@
         copy.start()
     for order in range(orders):
         load_weight(order).start()
+        load_peer_weight(order).start()
 
     send_group(groups - 1)
-    for row in range(lead, rows):
-        for step in range(1, chips):
-            chip_copy(step, row, chan_at, row - lead).start()
-    for index in range(4):
-        core_copy(slice(index * lead, (index + 1) * lead), chan_at).start()
+
+    @pl.when(has_behind)
+    def _():
+        via_copy().start()
+
+    part_copy(1 - chip, chan_at).start()
+    for row in range(lead, whole):
+        chip_copy(row, chan_at).start()
+    for index in range(0, whole, lead):
+        core_copy(slice(index, min(index + lead, whole)), chan_at).start()
+    core_part(chan_at).start()
 
     def forward(group, half):
         side_copy(group, half).wait_recv()
@@ -301,7 +350,10 @@
         def _():
             far_copy(half_of(half), cut_of(group), group).start()
 
-    forward(0, 0)
+    @pl.when(core == 1)
+    def _():
+        forward(0, 0)
+
     for copy in small:
         copy.wait()
     kin_high, kin_low = split_bf16(kin[...])
@@ -388,36 +440,51 @@
         )
         acc1[:, cut, :] = acc1[:, cut, :] + total.reshape(rows, GROUP, lanes)
 
-    def couple(row):
-        first_r = radius(row)
+    def factors_of(first_r):
         inverse = 1.0 / jnp.maximum(first_r, second_r)
         ratio = jnp.minimum(first_r, second_r) * inverse
         factors = [inverse]
         for _ in range(orders - 2):
             factors.append(factors[-1] * ratio)
         factors.append(field[0] * (first_r + second_r))
-        step = chans // 2
-        for first in range(0, chans, step):
-            total = jnp.zeros((step, lanes), jnp.float32)
-            for order in range(orders):
-                total = total + factors[order] * jnp.dot(
-                    weights[order, first : first + step, :],
-                    xg[row],
-                    preferred_element_type=jnp.float32,
-                )
-            acc[row, first : first + step, :] = acc[row, first : first + step, :] + total.astype(
-                jnp.bfloat16
-            ).astype(jnp.float32)
+        return factors
+
+    def summed(factors, matrices, source, some):
+        total = jnp.zeros((chans // 2, lanes), jnp.float32)
+        for order in range(orders):
+            total = total + factors[order] * jnp.dot(
+                matrices[order, some, :], source[...], preferred_element_type=jnp.float32
+            )
+        return total.astype(jnp.bfloat16)
+
+    cuts = (slice(0, chans // 2), slice(chans // 2, chans))
+
+    def couple(row):
+        factors = factors_of(radius(row))
+        for some in cuts:
+            total = summed(factors, weights, xg.at[row], some)
+            acc[row, some, :] = acc[row, some, :] + total.astype(jnp.float32)
+
+    def couple_parts(matrices, target):
+        place = lax.broadcasted_iota(jnp.int32, (1, lanes), 1) // width
+        place = place + (rad_at * rows + whole)
+        factors = factors_of(1.0 + 8.0 * place.astype(jnp.float32) / width)
+        for some in cuts:
+            target[some, :] = summed(factors, matrices, xp.at[chip], some)
+
+    def couple_peer():
+        couple_parts(peer_weights, back)
+
+    def couple_own():
+        back_copy(chip).start()
+        couple_parts(weights, coupled.at[chip])
 
     def relay(row):
-        for step in range(1, chips):
-            chip_copy(step, row, chip_source(step), row - lead).wait_recv()
-            relay_copy(step, row, chip_source(step), row - lead).start()
+        chip_copy(row, peer).wait_recv()
+        relay_copy(row, peer).start()
 
     def take_row(row):
-        for step in range(1, chips):
-            owner = chip_source(step) + 1 - 2 * core
-            relay_copy(step, row, owner, row - lead).wait_recv()
+        relay_copy(row, peer + 1 - 2 * core).wait_recv()
         couple(row)
 
     def take_side(group):
@@ -427,11 +494,21 @@
 
         side_group(group)
 
-    forward(0, 1)
+    def mix_slot(slot, cut):
+        value = halo[slot, :, cut, :].reshape(size, lanes)
+        total = mix(2 * slot, value).reshape(rows, GROUP, lanes)
+        acc1[:, cut, :] = acc1[:, cut, :] + total
+
+    @pl.when(core == 0)
+    def _():
+        forward(0, 0)
+
     for index in range(2):
         own_group(index)
-    for index in range(3):
+    for index in range(2):
         local_row(index)
+    forward(0, 1)
+    local_row(2)
 
     def phase(index, carry):
         for half in range(2):
@@ -442,31 +519,48 @@
                 local_row(index * 5 + half * 3 + place + 3)
         return carry
 
+    def merge(group, some_rows):
+        cut = cut_of(group)
+        targets = [out.at[1 - part].reshape(chans * rows, width) for part in range(2)]
+        for row in some_rows:
+            value = acc[row, cut, :] + acc1[row, cut, :]
+            place = (pl.ds(group * GROUP * rows + row, GROUP, stride=rows), slice(None))
+            for part in range(2):
+                piece = value[:, part * width : (part + 1) * width]
+                if row >= whole:
+                    lane = slice((row - whole) * width, (row - whole + 1) * width)
+                    piece = piece + coupled[part, cut, lane].astype(jnp.float32)
+                targets[part][place] = piece if part == 1 else -piece
+
+    def merge_groups(first, last, some_rows):
+        def step(group, carry):
+            merge(group, some_rows)
+            return carry
+
+        lax.fori_loop(first, last, step, 0)
+
     lax.fori_loop(0, 2, phase, 0)
-    for step in range(1, chips):
-        lead_copy(step, block(chip_source(step)), chip_source(step)).wait_recv()
-        relay_lead(step, chip_source(step)).start()
+    lead_copy(block(peer)).wait_recv()
+    relay_lead(peer).start()
     pltpu.make_async_copy(weights, weights, small_sem.at[2]).wait()
-    core_copy(every, partner).wait_recv()
+    pltpu.make_async_copy(peer_weights, peer_weights, small_sem.at[3]).wait()
+    core_copy(slice(0, whole), partner).wait_recv()
+    core_part(partner).wait_recv()
     for index in range(2):
         own_group(index + 10)
 
+    @pl.when(has_ahead)
+    def _():
+        via_copy().wait_recv()
+        via_forward().start()
+
     def main(index, carry):
         start = index * lead
 
-        def when_first(work, *args):
-            @pl.when(index == 1)
+        def at(turn, work, *args):
+            @pl.when(index == turn)
             def _():
                 work(*args)
-
-        def lead_or_row(row):
-            @pl.when(index == 1)
-            def _():
-                couple(row)
-
-            @pl.when(index > 1)
-            def _():
-                take_row(row)
 
         forward(3 * index, 0)
 
@@ -474,69 +568,88 @@
         def _():
             for row in range(13, rows):
                 local_row(row)
-            for step in range(1, chips):
-                relay_lead(step, chip_source(step) + 1 - 2 * core).wait_recv()
-
-        lead_or_row(start - 2)
+            part_copy(chip, peer).wait_recv()
+            relay_part(peer).start()
+            relay_lead(peer + 1 - 2 * core).wait_recv()
+            couple(0)
+
+        @pl.when(index > 1)
+        def _():
+            take_row(start - 2)
+            relay(start - 1)
+
         forward(3 * index, 1)
+        take_side(3 * index - 3)
+        at(1, couple, 1)
+
+        @pl.when(index == 2)
+        def _():
+            relay_part(peer + 1 - 2 * core).wait_recv()
+            couple_peer()
+
+        forward(3 * index + 1, 0)
         relay(start)
         take_side(3 * index - 2)
-        lead_or_row(start - 1)
-        forward(3 * index + 1, 0)
-        relay(start + 1)
-        take_side(3 * index - 1)
-        when_first(take_side, 0)
-        when_first(couple, 0)
+        at(1, couple, 2)
+
+        @pl.when(index > 1)
+        def _():
+            take_row(start - 1)
+
         forward(3 * index + 1, 1)
         take_row(start)
+        relay(start + 1)
         forward(3 * index + 2, 0)
-        relay(start + 2)
-        take_row(start + 1)
-        forward(3 * index + 2, 1)
-        relay(start + 3)
-        take_side(3 * index)
-        when_first(couple, 1)
+        take_side(3 * index - 1)
+        at(1, couple, 3)
+        at(2, couple_own)
+        at(3, merge_groups, 0, groups - 3, range(whole - 1))
+
+        @pl.when(index < 3)
+        def _():
+            forward(3 * index + 2, 1)
+            relay(start + 2)
+            take_row(start + 1)
+
         return carry
 
     lax.fori_loop(1, 4, main, 0)
 
-    def merge(group, some_rows):
-        cut = cut_of(group)
-        first = out.at[0].reshape(chans * rows, width)
-        second = out.at[1].reshape(chans * rows, width)
-        for row in some_rows:
-            value = acc[row, cut, :] + acc1[row, cut, :]
-            place = (pl.ds(group * GROUP * rows + row, GROUP, stride=rows), slice(None))
-            first[place] = value[:, width:]
-            second[place] = -value[:, :width]
-
-    def merge_most(group, carry):
-        merge(group, range(rows - 1))
-        return carry
-
-    def merge_last(group, carry):
-        merge(group, range(rows - 1, rows))
-        return carry
-
-    take_row(rows - 2)
-    lax.fori_loop(0, groups - 2, merge_most, 0)
+    take_side(groups - 3)
+    take_row(whole - 1)
+    merge_groups(0, groups - 3, range(whole - 1, whole))
+    merge(groups - 3, range(whole))
+    back_copy(1 - chip).wait_recv()
+    merge_groups(0, groups - 2, range(whole, rows))
     take_side(groups - 2)
-    merge(groups - 2, range(rows - 1))
-    take_row(rows - 1)
-    lax.fori_loop(0, groups - 1, merge_last, 0)
-    take_side(groups - 1)
+    merge(groups - 2, range(rows))
+    side_copy(groups - 1, 1).wait_recv()
+    mix_slot(near_slot, cut_of(groups - 1))
+
+    @pl.when(has_behind)
+    def _():
+        far_copy(half_of(0), cut_of(groups - 1), groups - 1).wait_recv()
+        via_forward().wait_recv()
+
+    mix_slot(far_slot, cut_of(groups - 1))
     merge(groups - 1, range(rows))
 
-    core_copy(every, chan_at).wait_send()
-    for step in range(1, chips):
-        lead_copy(step, block(chan_at), chan_at).wait_send()
-        chip_copy(step, slice(lead, rows), chan_at, 0).wait_send()
-        relay_copy(step, every, chip_source(step), 0).wait_send()
-    remote(xg.at[:, block(chan_at), :], halo.at[minor], ys, yr.at[0, 0], {"rad": other}).wait_send()
+    core_copy(slice(0, whole), chan_at).wait_send()
+    core_part(chan_at).wait_send()
+    sent(lead, hs, {"chan": peer})
+    sent(rows - lead, xs, {"chan": peer})
+    sent(rows - 1, fs, {"chan": partner})
+    sent(rows, ys, {"rad": other})
 
     @pl.when(has_ahead)
     def _():
-        far_copy(every, slice(0, chans), 0).wait_send()
+        view = xg.at[0 : rows // 2, 0 : (2 * groups - 1) * GROUP, :]
+        remote(view, view, zs, zr.at[0], {"rad": ahead}).wait_send()
+        via_forward().wait_send()
+
+    @pl.when(has_behind)
+    def _():
+        via_copy().wait_send()
 
 
 def device_step(peers, rads, psi, k_prev, gaunt, dipole, kinetic, chan_l, field_amp):
@@ -544,7 +657,7 @@
     fits = (
         chans == 3 * 4 * GROUP
         and rows == GROUP
-        and peers % 2 == 0
+        and peers == 4
         and rads % 2 == 0
         and width == rads * rows
         and width == 128
@@ -571,33 +684,39 @@
         scratch_shapes=[
             pltpu.VMEM(kinetic.shape, f32),
             pltpu.VMEM((2, chans), jnp.int32),
-            pltpu.VMEM((2, chans, rows, width), f32),
-            pltpu.VMEM((2, chans, rows, width), f32),
+            pltpu.VMEM((2, 2, chans, rows, width), f32),
             pltpu.VMEM((rows, chans, lanes), f32),
             pltpu.VMEM((rows, peers * chans, lanes), bf16),
+            pltpu.VMEM((2, peers * chans, lanes), bf16),
+            pltpu.VMEM((2, chans, lanes), bf16),
+            pltpu.VMEM((chans, lanes), bf16),
             pltpu.VMEM((2, rows, chans, lanes), bf16),
             pltpu.VMEM((rows, chans, lanes), f32),
             pltpu.VMEM((rows, chans, lanes), f32),
+            pltpu.VMEM((orders, chans, peers * chans), bf16),
             pltpu.VMEM((orders, chans, peers * chans), bf16),
             pltpu.VMEM((3, 2 * size, size), bf16),
             pltpu.VMEM((lanes, lanes), bf16),
             pltpu.VMEM((chans, width), f32),
             pltpu.VMEM((chans, width), f32),
-            dma((2, len(LOADS))),
-            dma((3,)),
-            dma((chips - 1,)),
-            dma((chips - 1,)),
-            dma((chips - 1,)),
-            dma((chips - 1, rows - rows // 4)),
+            dma((len(LOADS),)),
+            dma((4,)),
             dma,
             dma,
-            dma((chips - 1,)),
-            dma((chips - 1,)),
-            dma((chips - 1, rows - rows // 4)),
+            dma,
+            dma((rows - rows // 4,)),
+            dma,
+            dma((2,)),
+            dma,
+            dma,
+            dma((rows - rows // 4 - 1,)),
             dma,
             dma((2, groups)),
             dma,
             dma((groups,)),
+            dma((2,)),
+            dma((2,)),
+            pltpu.VMEM((rows // 2, GROUP, lanes), bf16),
         ],
         compiler_params=pltpu.CompilerParams(
             collective_id=0, has_side_effects=True, vmem_limit_bytes=36 * 1024 * 1024

time: 45.9 us -> 45.1 us (0.983)
  Pallas kernels: 43.4 us -> 42.6 us
    pallas_call x1, Pallas kernels: 43.4 us -> 42.6 us  [device_step(): pl.pallas_call(functools.partial(fused_kernel, peers, rads), out_shape=ja...]
where the time goes in v2:
time: 45.1 us; the launch traced here: 45 us
  Pallas kernels  42.6 us (94%)
  local copies, waits for them, and re-layouts  1.67 us (4%)
  between operations  0.66 us (1%)
    pallas_call x1, Pallas kernels, device_step(): pl.pallas_call(functools.partial(fused_kernel, peers, rads), out_shape=ja...  42.6 us
    unnamed x1, local copies, waits for them, and re-layouts  1.67 us

profile of v2, /device:TPU:0, one launch (start us, length us, event | category | flops | bytes accessed | tf_op | source)
XLA Modules:
  0.0 45.0 jit_solution(9919575743492633806)
XLA Ops:
  0.7 42.6 %shard_map.73 = f32[2,192,16,128]{3,2,1,0:T(8,128)S(1)} custom-call(f32[2,192,16,128]{3,2,1,0:T(8,128)} %psi.1, f32[2,192,16,128]{3,2,1,0:T(8,128)} %k_prev.1, bf16[4,768,768]{2,1,0:T(8,128)(2,1)} %gaunt.1, bf16[768,768]{1,0:T(8,128)(2,1)} %dipole.1, f32[128,128]{1,0:T(8,128)} %kin_main.1, s32[2,192]{1,0:T(2,128)} %bitcast.1, f32[1]{0:T(128)S(6)} %copy.9.field), custom_call_target="tpu_custom_call" | custom-call | tf_op jit(solution)/shard_map/pallas_call | solution.py:679
  43.3 1.7 %copy.10 = f32[2,192,16,128]{3,2,1,0:T(8,128)} copy(f32[2,192,16,128]{3,2,1,0:T(8,128)S(1)} %shard_map.73) | data formatting | bytes 6291456

commit v3 on v2

--- a/solution.py
+++ b/solution.py
@@ -76,12 +76,45 @@
 
 MESH = pl.DeviceIdType.MESH
 GROUP = 16
-LOADS = ((0, 1), (1, 2), (2, 4), (4, 8), (8, 12))
+LOADS = ((0, 1), (1, 4), (4, 12))
 
 
 def split_bf16(value):
     high = value.astype(jnp.bfloat16)
     return high, (value - high.astype(jnp.float32)).astype(jnp.bfloat16)
+
+
+def merge(acc, target, group, some_rows):
+    width = acc.shape[2] // 2
+    chans, height = target.shape[1:3]
+    cut = pl.ds(pl.multiple_of(group * GROUP, GROUP), GROUP)
+    views = [target.at[part].reshape(chans * height, width) for part in range(2)]
+    for row in some_rows:
+        value = acc[row, cut, :]
+        place = (pl.ds(group * GROUP * height + row, GROUP, stride=height), slice(None))
+        views[0][place] = value[:, width:]
+        views[1][place] = -value[:, :width]
+
+
+def finish_kernel(acc, top, out, whole, sem):
+    rows, chans, _ = acc.shape
+    upper = rows // 2
+    done = chans - 2 * GROUP
+
+    def store(source, cut, some_rows):
+        return pltpu.make_async_copy(source, out.at[:, cut, some_rows, :], sem)
+
+    store(top.at[:, 0:done], slice(0, done), slice(0, upper)).start()
+    for first in range(0, done, 2 * GROUP):
+        for group in range(first // GROUP, first // GROUP + 2):
+            merge(acc, whole, group, range(upper, rows))
+        cut, low = (slice(first, first + 2 * GROUP), slice(upper, rows))
+        store(whole.at[:, cut, low, :], cut, low).start()
+    for group in range(done // GROUP, chans // GROUP):
+        merge(acc, whole, group, range(rows))
+    cut = slice(done, chans)
+    store(whole.at[:, cut], cut, slice(0, rows)).start()
+    pltpu.make_async_copy(whole, out, sem).wait()
 
 
 def fused_kernel(
@@ -94,7 +127,8 @@
     kin_main,
     chan_main,
     field,
-    out,
+    acc,
+    top,
     kin,
     chan_l,
     pk,
@@ -104,8 +138,6 @@
     coupled,
     back,
     halo,
-    acc,
-    acc1,
     weights,
     peer_weights,
     wr1,
@@ -321,6 +353,7 @@
         send_group(group - 1)
         return carry
 
+    lax.fori_loop(2, LOADS[1][1], form_next, 0)
     for part in range(2, len(LOADS)):
         arrive(part)
         lax.fori_loop(LOADS[part][0], LOADS[part][1], form_next, 0)
@@ -343,16 +376,22 @@
         core_copy(slice(index, min(index + lead, whole)), chan_at).start()
     core_part(chan_at).start()
 
-    def forward(group, half):
+    def pass_on(group, half):
         side_copy(group, half).wait_recv()
-
-        @pl.when(has_ahead)
+        last = jnp.logical_and(group == groups - 1, half == 1)
+
+        @pl.when(jnp.logical_and(has_ahead, jnp.logical_not(last)))
         def _():
             far_copy(half_of(half), cut_of(group), group).start()
 
+    def forward(group, half):
+        @pl.when(group + core < groups)
+        def _():
+            pass_on(group + core, half)
+
     @pl.when(core == 1)
     def _():
-        forward(0, 0)
+        pass_on(0, 0)
 
     for copy in small:
         copy.wait()
@@ -379,6 +418,10 @@
                 jnp.bfloat16
             )
 
+    @pl.when(core == 1)
+    def _():
+        pass_on(0, 1)
+
     @pl.when(jnp.logical_not(has_behind))
     def _():
         halo[far_slot] = jnp.zeros(halo.shape[1:], halo.dtype)
@@ -415,7 +458,8 @@
             both = jnp.dot(
                 jnp.concatenate([high, low], axis=1), kk[...], preferred_element_type=jnp.float32
             )
-            acc[row, :, cut] = both[:, :width] + both[:, width:] + potential * value
+            total = both[:, :width] + both[:, width:] + potential * value
+            acc[row, :, cut] = acc[row, :, cut] + total
 
     def mix(side, value):
         both = jnp.dot(wr1[side], value, preferred_element_type=jnp.float32)
@@ -430,7 +474,7 @@
         total = mix(1, high) + jnp.dot(
             wr1[1, 0:size, :], low, preferred_element_type=jnp.float32
         )
-        acc1[:, pl.ds(first, GROUP), :] = total.reshape(rows, GROUP, lanes)
+        acc[:, pl.ds(first, GROUP), :] = total.reshape(rows, GROUP, lanes)
 
     def side_group(index):
         first = pl.multiple_of(index * GROUP, GROUP)
@@ -438,7 +482,7 @@
         total = mix(0, halo[0, :, cut, :].reshape(size, lanes)) + mix(
             2, halo[1, :, cut, :].reshape(size, lanes)
         )
-        acc1[:, cut, :] = acc1[:, cut, :] + total.reshape(rows, GROUP, lanes)
+        acc[:, cut, :] = acc[:, cut, :] + total.reshape(rows, GROUP, lanes)
 
     def factors_of(first_r):
         inverse = 1.0 / jnp.maximum(first_r, second_r)
@@ -473,18 +517,26 @@
             target[some, :] = summed(factors, matrices, xp.at[chip], some)
 
     def couple_peer():
+        relay_part(peer + 1 - 2 * core).wait_recv()
         couple_parts(peer_weights, back)
 
     def couple_own():
         back_copy(chip).start()
         couple_parts(weights, coupled.at[chip])
 
-    def relay(row):
-        chip_copy(row, peer).wait_recv()
-        relay_copy(row, peer).start()
+    def relay(base):
+        row = base + core
+
+        @pl.when(jnp.logical_and(row >= lead, row < whole))
+        def _():
+            chip_copy(row, peer).wait_recv()
+            relay_copy(row, peer).start()
 
     def take_row(row):
-        relay_copy(row, peer + 1 - 2 * core).wait_recv()
+        @pl.when(row >= lead)
+        def _():
+            relay_copy(row, peer + 1 - 2 * core).wait_recv()
+
         couple(row)
 
     def take_side(group):
@@ -497,57 +549,40 @@
     def mix_slot(slot, cut):
         value = halo[slot, :, cut, :].reshape(size, lanes)
         total = mix(2 * slot, value).reshape(rows, GROUP, lanes)
-        acc1[:, cut, :] = acc1[:, cut, :] + total
-
-    @pl.when(core == 0)
-    def _():
-        forward(0, 0)
-
-    for index in range(2):
-        own_group(index)
-    for index in range(2):
-        local_row(index)
+        acc[:, cut, :] = acc[:, cut, :] + total
+
+    def each_of(first, last, work):
+        def step(index, carry):
+            work(index)
+            return carry
+
+        lax.fori_loop(first, last, step, 0)
+
+    def merge_top(first, last):
+        each_of(first, last, lambda group: merge(acc, top, group, range(rows // 2)))
+
+    def take_lead(turn):
+        @pl.when(core == turn)
+        def _():
+            lead_copy(block(peer)).wait_recv()
+            relay_lead(peer).start()
+
+    forward(0, 0)
+    each_of(0, 3, own_group)
     forward(0, 1)
-    local_row(2)
-
-    def phase(index, carry):
-        for half in range(2):
-            forward(index + 1, half)
-            for place in range(2):
-                own_group(index * 4 + half * 2 + place + 2)
-            for place in range(3 - half):
-                local_row(index * 5 + half * 3 + place + 3)
-        return carry
-
-    def merge(group, some_rows):
-        cut = cut_of(group)
-        targets = [out.at[1 - part].reshape(chans * rows, width) for part in range(2)]
-        for row in some_rows:
-            value = acc[row, cut, :] + acc1[row, cut, :]
-            place = (pl.ds(group * GROUP * rows + row, GROUP, stride=rows), slice(None))
-            for part in range(2):
-                piece = value[:, part * width : (part + 1) * width]
-                if row >= whole:
-                    lane = slice((row - whole) * width, (row - whole + 1) * width)
-                    piece = piece + coupled[part, cut, lane].astype(jnp.float32)
-                targets[part][place] = piece if part == 1 else -piece
-
-    def merge_groups(first, last, some_rows):
-        def step(group, carry):
-            merge(group, some_rows)
-            return carry
-
-        lax.fori_loop(first, last, step, 0)
-
-    lax.fori_loop(0, 2, phase, 0)
-    lead_copy(block(peer)).wait_recv()
-    relay_lead(peer).start()
+    each_of(3, 4, own_group)
+    for half in range(2):
+        forward(1, half)
+        each_of(4 + 4 * half, 8 + 4 * half, own_group)
+    for half in range(2):
+        forward(2, half)
+        take_lead(1 - half)
+        each_of(6 * half, 6 + 6 * half, local_row)
     pltpu.make_async_copy(weights, weights, small_sem.at[2]).wait()
     pltpu.make_async_copy(peer_weights, peer_weights, small_sem.at[3]).wait()
     core_copy(slice(0, whole), partner).wait_recv()
     core_part(partner).wait_recv()
-    for index in range(2):
-        own_group(index + 10)
+    each_of(12, rows - 1, local_row)
 
     @pl.when(has_ahead)
     def _():
@@ -557,74 +592,63 @@
     def main(index, carry):
         start = index * lead
 
-        def at(turn, work, *args):
-            @pl.when(index == turn)
+        def each(first, second):
+            return (1 - core) * first + core * second
+
+        def when(condition, work, *args):
+            @pl.when(condition)
             def _():
                 work(*args)
 
+        even, odd = (core == 0, core == 1)
+        started, ended = (index == 1, index == 3)
         forward(3 * index, 0)
 
-        @pl.when(index == 1)
+        @pl.when(started)
         def _():
-            for row in range(13, rows):
-                local_row(row)
             part_copy(chip, peer).wait_recv()
             relay_part(peer).start()
+            local_row(rows - 1)
             relay_lead(peer + 1 - 2 * core).wait_recv()
-            couple(0)
-
-        @pl.when(index > 1)
-        def _():
-            take_row(start - 2)
-            relay(start - 1)
-
+
+        when(jnp.logical_or(odd, index != 2), take_row, each(index - 1, start - 2))
+        when(jnp.logical_and(even, index == 2), couple_peer)
+        relay(start - 1)
         forward(3 * index, 1)
-        take_side(3 * index - 3)
-        at(1, couple, 1)
-
-        @pl.when(index == 2)
-        def _():
-            relay_part(peer + 1 - 2 * core).wait_recv()
-            couple_peer()
-
+        take_side(3 * index - 2)
+        when(jnp.logical_or(even, started), take_row, each(start - 1, 0))
+        when(jnp.logical_and(odd, index == 2), couple_peer)
         forward(3 * index + 1, 0)
         relay(start)
-        take_side(3 * index - 2)
-        at(1, couple, 2)
-
-        @pl.when(index > 1)
-        def _():
-            take_row(start - 1)
-
+        take_row(start - core)
+        when(ended, merge_top, 0, groups - 4)
+        when(started, take_side, 0)
         forward(3 * index + 1, 1)
-        take_row(start)
+        when(jnp.logical_or(odd, started), take_row, each(1, start))
+        when(jnp.logical_and(even, index == 2), couple_own)
+        take_side(3 * index - 1)
         relay(start + 1)
         forward(3 * index + 2, 0)
-        take_side(3 * index - 1)
-        at(1, couple, 3)
-        at(2, couple_own)
-        at(3, merge_groups, 0, groups - 3, range(whole - 1))
-
-        @pl.when(index < 3)
-        def _():
-            forward(3 * index + 2, 1)
-            relay(start + 2)
-            take_row(start + 1)
-
+        when(jnp.logical_or(even, started), take_row, each(start + 1, 1))
+        when(jnp.logical_and(odd, index == 2), couple_own)
+        when(index < 3, forward, 3 * index + 2, 1)
+        relay(start + 2)
+        take_side(3 * index)
+        when(start + 2 - core < whole, take_row, start + 2 - core)
         return carry
 
     lax.fori_loop(1, 4, main, 0)
 
-    take_side(groups - 3)
-    take_row(whole - 1)
-    merge_groups(0, groups - 3, range(whole - 1, whole))
-    merge(groups - 3, range(whole))
+    merge_top(groups - 4, groups - 2)
     back_copy(1 - chip).wait_recv()
-    merge_groups(0, groups - 2, range(whole, rows))
+    for place in range(rows - whole):
+        for part in range(2):
+            lane = slice(part * width, (part + 1) * width)
+            value = coupled[part, :, place * width : (place + 1) * width].astype(jnp.float32)
+            acc[whole + place, :, lane] = acc[whole + place, :, lane] + value
+    forward(groups - 1, 1)
+    mix_slot(near_slot, cut_of(groups - 1))
     take_side(groups - 2)
-    merge(groups - 2, range(rows))
-    side_copy(groups - 1, 1).wait_recv()
-    mix_slot(near_slot, cut_of(groups - 1))
 
     @pl.when(has_behind)
     def _():
@@ -632,7 +656,6 @@
         via_forward().wait_recv()
 
     mix_slot(far_slot, cut_of(groups - 1))
-    merge(groups - 1, range(rows))
 
     core_copy(slice(0, whole), chan_at).wait_send()
     core_part(chan_at).wait_send()
@@ -672,15 +695,17 @@
     f32, bf16, dma = (jnp.float32, jnp.bfloat16, pltpu.SemaphoreType.DMA)
     main_memory = pl.BlockSpec(memory_space=pltpu.HBM)
     vmem = pl.BlockSpec(memory_space=pltpu.VMEM)
+    summed = jax.ShapeDtypeStruct((rows, chans, lanes), f32)
+    top = jax.ShapeDtypeStruct((2, chans, rows // 2, width), f32)
     psi, k_prev, gaunt, dipole, kinetic, chan_l = (
         pltpu.with_memory_space_constraint(value, pltpu.HBM)
         for value in (psi, k_prev, gaunt, dipole, kinetic, chan_l.T)
     )
-    return pl.pallas_call(
+    parts = pl.pallas_call(
         functools.partial(fused_kernel, peers, rads),
-        out_shape=jax.ShapeDtypeStruct(psi.shape, f32),
+        out_shape=(summed, top),
         in_specs=[main_memory] * 6 + [pl.BlockSpec(memory_space=pltpu.SMEM)],
-        out_specs=vmem,
+        out_specs=(vmem, vmem),
         scratch_shapes=[
             pltpu.VMEM(kinetic.shape, f32),
             pltpu.VMEM((2, chans), jnp.int32),
@@ -691,8 +716,6 @@
             pltpu.VMEM((2, chans, lanes), bf16),
             pltpu.VMEM((chans, lanes), bf16),
             pltpu.VMEM((2, rows, chans, lanes), bf16),
-            pltpu.VMEM((rows, chans, lanes), f32),
-            pltpu.VMEM((rows, chans, lanes), f32),
             pltpu.VMEM((orders, chans, peers * chans), bf16),
             pltpu.VMEM((orders, chans, peers * chans), bf16),
             pltpu.VMEM((3, 2 * size, size), bf16),
@@ -722,6 +745,14 @@
             collective_id=0, has_side_effects=True, vmem_limit_bytes=36 * 1024 * 1024
         ),
     )(psi, k_prev, gaunt, dipole, kinetic, chan_l, field_amp)
+    return pl.pallas_call(
+        finish_kernel,
+        out_shape=jax.ShapeDtypeStruct(psi.shape, f32),
+        in_specs=[vmem, vmem],
+        out_specs=main_memory,
+        scratch_shapes=[pltpu.VMEM(psi.shape, f32), dma],
+        compiler_params=pltpu.CompilerParams(vmem_limit_bytes=8 * 1024 * 1024),
+    )(*parts)
 
 
 def solution(mesh):

time: 45.1 us -> 43.6 us (0.967)
  local copies, waits for them, and re-layouts: 1.67 us -> 0 us
    unnamed x1 -> x0, local copies, waits for them, and re-layouts: 1.67 us -> none
    pallas_call x1 -> x2, Pallas kernels: 42.6 us -> 42.5 us  [the longest x1 40.9 us: device_step(): pl.pallas_call(functools.partial(fused_kernel, peers, rads), out_shape=(s...]
where the time goes in v3:
time: 43.6 us; the launch traced here: 43.2 us
  Pallas kernels  42.5 us (97%)
  between operations  0.66 us (2%)
    pallas_call x1, Pallas kernels, device_step(): pl.pallas_call(functools.partial(fused_kernel, peers, rads), out_shape=(s...  40.9 us
    pallas_call x1, Pallas kernels, device_step(): pl.pallas_call(finish_kernel, out_shape=jax.ShapeDtypeStruct(psi.shape, f...  1.67 us

profile of v3, /device:TPU:0, one launch (start us, length us, event | category | flops | bytes accessed | tf_op | source)
XLA Modules:
  0.0 43.2 jit_solution(6370912983926201434)
XLA Ops:
  0.7 40.9 %shard_map.73 = (f32[16,192,256]{2,1,0:T(8,128)S(1)}, f32[2,192,8,128]{3,2,1,0:T(8,128)S(1)}) custom-call(f32[2,192,16,128]{3,2,1,0:T(8,128)} %psi.1, f32[2,192,16,128]{3,2,1,0:T(8,128)} %k_prev.1, bf16[4,768,768]{2,1,0:T(8,128)(2,1)} %gaunt.1, bf16[768,768]{1,0:T(8,128)(2,1)} %dipole.1, f32[128,128]{1,0:T(8,128)} %kin_main.1, s32[2,192]{1,0:T(2,128)} %bitcast.1, ...), custom_call_target="tpu_custom_call" | custom-call | tf_op jit(solution)/shard_map/pallas_call | solution.py:704
  41.5 1.7 %shard_map.74 = f32[2,192,16,128]{3,2,1,0:T(8,128)} custom-call(f32[16,192,256]{2,1,0:T(8,128)S(1)} %get-tuple-element.7.acc, f32[2,192,8,128]{3,2,1,0:T(8,128)S(1)} %get-tuple-element.8.top), custom_call_target="tpu_custom_call" | custom-call | tf_op jit(solution)/shard_map/pallas_call | solution.py:748

commit v4 on v3

--- a/solution.py
+++ b/solution.py
@@ -76,6 +76,8 @@
 
 MESH = pl.DeviceIdType.MESH
 GROUP = 16
+PAIRS = 2
+TAIL = 2
 LOADS = ((0, 1), (1, 4), (4, 12))
 
 
@@ -84,37 +86,42 @@
     return high, (value - high.astype(jnp.float32)).astype(jnp.bfloat16)
 
 
-def merge(acc, target, group, some_rows):
-    width = acc.shape[2] // 2
-    chans, height = target.shape[1:3]
-    cut = pl.ds(pl.multiple_of(group * GROUP, GROUP), GROUP)
-    views = [target.at[part].reshape(chans * height, width) for part in range(2)]
-    for row in some_rows:
-        value = acc[row, cut, :]
-        place = (pl.ds(group * GROUP * height + row, GROUP, stride=height), slice(None))
-        views[0][place] = value[:, width:]
-        views[1][place] = -value[:, :width]
-
-
-def finish_kernel(acc, top, out, whole, sem):
-    rows, chans, _ = acc.shape
-    upper = rows // 2
-    done = chans - 2 * GROUP
-
-    def store(source, cut, some_rows):
-        return pltpu.make_async_copy(source, out.at[:, cut, some_rows, :], sem)
-
-    store(top.at[:, 0:done], slice(0, done), slice(0, upper)).start()
-    for first in range(0, done, 2 * GROUP):
-        for group in range(first // GROUP, first // GROUP + 2):
-            merge(acc, whole, group, range(upper, rows))
-        cut, low = (slice(first, first + 2 * GROUP), slice(upper, rows))
-        store(whole.at[:, cut, low, :], cut, low).start()
-    for group in range(done // GROUP, chans // GROUP):
-        merge(acc, whole, group, range(rows))
-    cut = slice(done, chans)
-    store(whole.at[:, cut], cut, slice(0, rows)).start()
-    pltpu.make_async_copy(whole, out, sem).wait()
+def lay_out(target, group, row, value):
+    _, chans, height, width = target.shape
+    place = (pl.ds(group * GROUP * height + row, GROUP, stride=height), slice(None))
+    target.at[0].reshape(chans * height, width)[place] = value[:, width:]
+    target.at[1].reshape(chans * height, width)[place] = -value[:, :width]
+
+
+def finish_kernel(rads, acc, early, far_tail, wr1, out, late, sem):
+    rows, chans, lanes = acc.shape
+    size = rows * GROUP
+    done = chans - TAIL * GROUP
+    rad_at = lax.axis_index("rad")
+    minor = rad_at % 2
+    behind = rad_at - 2 + 4 * minor
+    has_behind = jnp.logical_and(behind >= 0, behind < rads)
+    pltpu.make_async_copy(early.at[:, 0:done], out.at[:, 0:done], sem).start()
+
+    for group in range(TAIL):
+        cut = slice(group * GROUP, (group + 1) * GROUP)
+        there = slice(done + group * GROUP, done + (group + 1) * GROUP)
+
+        @pl.when(has_behind)
+        def _():
+            value = far_tail[:, cut, :].reshape(size, lanes)
+            both = jnp.dot(wr1[2 * minor], value, preferred_element_type=jnp.float32)
+            total = (both[:size] + both[size:]).reshape(rows, GROUP, lanes)
+            for row in range(rows):
+                lay_out(late, group, row, acc[row, there, :] + total[row])
+
+        @pl.when(jnp.logical_not(has_behind))
+        def _():
+            for row in range(rows):
+                lay_out(late, group, row, acc[row, there, :])
+
+        pltpu.make_async_copy(late.at[:, cut], out.at[:, there], sem).start()
+    pltpu.make_async_copy(early, out, sem).wait()
 
 
 def fused_kernel(
@@ -128,7 +135,9 @@
     chan_main,
     field,
     acc,
-    top,
+    early,
+    far_tail,
+    wr1,
     kin,
     chan_l,
     pk,
@@ -136,26 +145,19 @@
     xg,
     xp,
     coupled,
-    back,
     halo,
     weights,
-    peer_weights,
-    wr1,
     kk,
     lmul,
     langle,
     load_sem,
     small_sem,
-    hs,
     hr,
     xs,
     xr,
-    cs,
     cr,
-    fs,
     fl,
     fr,
-    ys,
     yr,
     zs,
     zr,
@@ -165,7 +167,7 @@
 ):
     rows, chans, lanes = sec.shape
     width = lanes // 2
-    orders = weights.shape[0]
+    orders = weights.shape[1]
     chips = peers // 2
     groups = chans // GROUP
     lead = rows // 4
@@ -182,7 +184,8 @@
     has_behind = jnp.logical_and(behind >= 0, behind < rads)
     near_slot = 1 - minor
     far_slot = minor
-    whole = rows - 2
+    whole = rows - 2 * PAIRS
+    back = 2
     peer = lax.rem(chip + 1, chips) * 2 + core
 
     def block(owner):
@@ -212,16 +215,11 @@
         view = pk.at[:, :, first * GROUP : last * GROUP, :, :]
         pltpu.make_async_copy(view, view, load_sem.at[part]).wait()
 
-    def load_weight(order):
+    def load_weight(kind, order):
         source = gaunt.at[order] if order < orders - 1 else dipole
+        owner = (peer, chan_at)[kind]
         return pltpu.make_async_copy(
-            source.at[block(chan_at), :], weights.at[order], small_sem.at[2]
-        )
-
-    def load_peer_weight(order):
-        source = gaunt.at[order] if order < orders - 1 else dipole
-        return pltpu.make_async_copy(
-            source.at[block(peer), :], peer_weights.at[order], small_sem.at[3]
+            source.at[block(owner), :], weights.at[kind, order], small_sem.at[2]
         )
 
     def remote(source, target, send, recv, device):
@@ -236,42 +234,39 @@
 
     def lead_copy(some):
         view = xg.at[0:lead, some, :]
-        return remote(view, view, hs, hr, {"chan": peer})
+        return remote(view, view, xs, hr, {"chan": peer})
 
     def chip_copy(row, owner):
         view = xg.at[row, block(owner), :]
         return remote(view, view, xs, xr.at[row - lead], {"chan": peer})
 
     def part_copy(part, owner):
-        view = xp.at[part, block(owner), :]
+        view = xp.at[part, :, block(owner), :]
         return remote(view, view, xs, xr.at[whole - lead], {"chan": peer})
 
     def back_copy(part):
-        return remote(back, coupled.at[part], xs, xr.at[whole - lead + 1], {"chan": peer})
+        source, target = (coupled.at[back], coupled.at[part])
+        return remote(source, target, xs, xr.at[whole - lead + 1], {"chan": peer})
 
     def core_copy(some_rows, owner):
         view = xg.at[some_rows, block(owner), :]
-        return remote(view, view, cs, cr.at[0], {"chan": partner})
+        return remote(view, view, xs, cr, {"chan": partner})
 
     def core_part(owner):
-        view = xp.at[chip, block(owner), :]
-        return remote(view, view, cs, cr.at[1], {"chan": partner})
+        view = xp.at[chip, :, block(owner), :]
+        return remote(view, view, xs, cr, {"chan": partner})
 
     def relay_lead(owner):
         view = xg.at[0:lead, block(owner), :]
-        return remote(view, view, fs, fl, {"chan": partner})
+        return remote(view, view, xs, fl, {"chan": partner})
 
     def relay_copy(row, owner):
         view = xg.at[row, block(owner), :]
-        return remote(view, view, fs, fr.at[row - lead], {"chan": partner})
+        return remote(view, view, xs, fr.at[row - lead], {"chan": partner})
 
     def relay_part(owner):
-        view = xp.at[chip, block(owner), :]
-        return remote(view, view, fs, fr.at[whole - lead], {"chan": partner})
-
-    def sent(count, sem, device):
-        view = xg.at[0:count, block(chan_at), :]
-        remote(view, view, sem, fl, device).wait_send()
+        view = xp.at[chip, :, block(owner), :]
+        return remote(view, view, xs, fr.at[whole - lead], {"chan": partner})
 
     def half_of(half):
         return slice(half * (rows // 2), (half + 1) * (rows // 2))
@@ -279,20 +274,35 @@
     def side_copy(group, half):
         source = xg.at[half_of(half), block_cut(chan_at, group), :]
         target = halo.at[minor, half_of(half), cut_of(group), :]
-        return remote(source, target, ys, yr.at[half, group], {"rad": other})
+        return remote(source, target, xs, yr.at[half, group], {"rad": other})
 
     def far_copy(some_rows, some, place):
         source = halo.at[near_slot, some_rows, some, :]
         target = halo.at[minor, some_rows, some, :]
         return remote(source, target, zs, zr.at[place], {"rad": ahead})
 
-    def via_copy():
-        source = xg.at[half_of(1), block_cut(chan_at, groups - 1), :]
-        return remote(source, via, vs.at[0], vr.at[0], {"rad": behind})
-
-    def via_forward():
-        target = halo.at[near_slot, half_of(1), cut_of(groups - 1), :]
-        return remote(via, target, vs.at[1], vr.at[1], {"rad": other})
+    def tail_cut(group):
+        return pl.ds(pl.multiple_of((group - groups + TAIL) * GROUP, GROUP), GROUP)
+
+    def tail_copy(some_rows, group):
+        source = halo.at[near_slot, some_rows, cut_of(group), :]
+        target = far_tail.at[some_rows, tail_cut(group), :]
+        return remote(source, target, zs, zr.at[group], {"rad": ahead})
+
+    def via_copy(some_rows):
+        source = xg.at[some_rows, block_cut(chan_at, groups - 1), :]
+        return remote(source, via.at[some_rows], vs, vr.at[0], {"rad": behind})
+
+    def via_forward(some_rows):
+        target = far_tail.at[some_rows, tail_cut(groups - 1), :]
+        return remote(via.at[some_rows], target, zs, vr.at[1], {"rad": other})
+
+    def by_core(condition, work):
+        for at, some_rows in enumerate((every, half_of(1))):
+
+            @pl.when(jnp.logical_and(core == at, condition))
+            def _():
+                work(some_rows)
 
     every = slice(0, rows)
     small = [
@@ -331,8 +341,9 @@
                 rounded = value.astype(jnp.bfloat16)
                 xg[row, block_cut(chan_at, group), cut] = rounded
                 if row >= whole:
-                    lane = slice((row - whole) * width, (row - whole + 1) * width)
-                    xp[part, block_cut(chan_at, group), lane] = rounded
+                    pair, turn = divmod(row - whole, 2)
+                    lane = slice(turn * width, (turn + 1) * width)
+                    xp[part, pair, block_cut(chan_at, group), lane] = rounded
 
     def send_group(group):
         for half in range(2):
@@ -360,14 +371,12 @@
     for copy in small:
         copy.start()
     for order in range(orders):
-        load_weight(order).start()
-        load_peer_weight(order).start()
+        for kind in range(2):
+            load_weight(kind, order).start()
 
     send_group(groups - 1)
 
-    @pl.when(has_behind)
-    def _():
-        via_copy().start()
+    by_core(has_behind, lambda some_rows: via_copy(some_rows).start())
 
     part_copy(1 - chip, chan_at).start()
     for row in range(lead, whole):
@@ -378,11 +387,16 @@
 
     def pass_on(group, half):
         side_copy(group, half).wait_recv()
-        last = jnp.logical_and(group == groups - 1, half == 1)
-
-        @pl.when(jnp.logical_and(has_ahead, jnp.logical_not(last)))
+
+        @pl.when(jnp.logical_and(has_ahead, group < groups - TAIL))
         def _():
             far_copy(half_of(half), cut_of(group), group).start()
+
+        late = jnp.logical_and(group >= groups - TAIL, group < groups - 1 + core * (1 - half))
+
+        @pl.when(jnp.logical_and(has_ahead, late))
+        def _():
+            tail_copy(half_of(half), group).start()
 
     def forward(group, half):
         @pl.when(group + core < groups)
@@ -422,10 +436,6 @@
     def _():
         pass_on(0, 1)
 
-    @pl.when(jnp.logical_not(has_behind))
-    def _():
-        halo[far_slot] = jnp.zeros(halo.shape[1:], halo.dtype)
-
     second_r = 1.0 + 8.0 * (
         lax.broadcasted_iota(jnp.int32, (1, lanes), 1) % width
     ).astype(jnp.float32) / width
@@ -506,23 +516,28 @@
     def couple(row):
         factors = factors_of(radius(row))
         for some in cuts:
-            total = summed(factors, weights, xg.at[row], some)
+            total = summed(factors, weights.at[1], xg.at[row], some)
             acc[row, some, :] = acc[row, some, :] + total.astype(jnp.float32)
 
-    def couple_parts(matrices, target):
+    def couple_parts(kind, pair):
         place = lax.broadcasted_iota(jnp.int32, (1, lanes), 1) // width
-        place = place + (rad_at * rows + whole)
+        place = place + (rad_at * rows + whole + 2 * pair)
         factors = factors_of(1.0 + 8.0 * place.astype(jnp.float32) / width)
+        target = kind * chip + (1 - kind) * back
         for some in cuts:
-            target[some, :] = summed(factors, matrices, xp.at[chip], some)
-
-    def couple_peer():
-        relay_part(peer + 1 - 2 * core).wait_recv()
-        couple_parts(peer_weights, back)
-
-    def couple_own():
-        back_copy(chip).start()
-        couple_parts(weights, coupled.at[chip])
+            total = summed(factors, weights.at[kind], xp.at[chip, pair], some)
+            coupled[target, pair, some, :] = total
+
+    def take_parts(unit):
+        @pl.when(unit == 0)
+        def _():
+            relay_part(peer + 1 - 2 * core).wait_recv()
+
+        @pl.when(unit == PAIRS)
+        def _():
+            back_copy(chip).start()
+
+        couple_parts(unit // PAIRS, unit % PAIRS)
 
     def relay(base):
         row = base + core
@@ -543,8 +558,11 @@
         @pl.when(has_behind)
         def _():
             far_copy(every, cut_of(group), group).wait_recv()
-
-        side_group(group)
+            side_group(group)
+
+        @pl.when(jnp.logical_not(has_behind))
+        def _():
+            mix_slot(near_slot, cut_of(group))
 
     def mix_slot(slot, cut):
         value = halo[slot, :, cut, :].reshape(size, lanes)
@@ -558,8 +576,12 @@
 
         lax.fori_loop(first, last, step, 0)
 
-    def merge_top(first, last):
-        each_of(first, last, lambda group: merge(acc, top, group, range(rows // 2)))
+    def merge(first, last, some_rows):
+        def one(group):
+            for row in some_rows:
+                lay_out(early, group, row, acc[row, cut_of(group), :])
+
+        each_of(first, last, one)
 
     def take_lead(turn):
         @pl.when(core == turn)
@@ -579,18 +601,17 @@
         take_lead(1 - half)
         each_of(6 * half, 6 + 6 * half, local_row)
     pltpu.make_async_copy(weights, weights, small_sem.at[2]).wait()
-    pltpu.make_async_copy(peer_weights, peer_weights, small_sem.at[3]).wait()
-    core_copy(slice(0, whole), partner).wait_recv()
-    core_part(partner).wait_recv()
+    core_copy(slice(0, whole + PAIRS), partner).wait_recv()
     each_of(12, rows - 1, local_row)
 
-    @pl.when(has_ahead)
-    def _():
-        via_copy().wait_recv()
-        via_forward().start()
+    def pass_via(some_rows):
+        via_copy(some_rows).wait_recv()
+        via_forward(some_rows).start()
+
+    by_core(has_ahead, pass_via)
 
     def main(index, carry):
-        start = index * lead
+        start = index * lead - 1
 
         def each(first, second):
             return (1 - core) * first + core * second
@@ -606,73 +627,79 @@
 
         @pl.when(started)
         def _():
-            part_copy(chip, peer).wait_recv()
-            relay_part(peer).start()
             local_row(rows - 1)
             relay_lead(peer + 1 - 2 * core).wait_recv()
 
-        when(jnp.logical_or(odd, index != 2), take_row, each(index - 1, start - 2))
-        when(jnp.logical_and(even, index == 2), couple_peer)
+        when(jnp.logical_or(odd, started), take_row, each(0, start - 2))
+        when(jnp.logical_and(even, index > 1), take_parts, 2 * index - 4)
         relay(start - 1)
         forward(3 * index, 1)
         take_side(3 * index - 2)
         when(jnp.logical_or(even, started), take_row, each(start - 1, 0))
-        when(jnp.logical_and(odd, index == 2), couple_peer)
+        when(jnp.logical_and(odd, index > 1), take_parts, 2 * index - 3)
         forward(3 * index + 1, 0)
         relay(start)
+
+        @pl.when(started)
+        def _():
+            part_copy(chip, peer).wait_recv()
+            relay_part(peer).start()
+
         take_row(start - core)
-        when(ended, merge_top, 0, groups - 4)
         when(started, take_side, 0)
+        when(ended, merge, 0, groups - 4, range(rows // 2))
         forward(3 * index + 1, 1)
         when(jnp.logical_or(odd, started), take_row, each(1, start))
-        when(jnp.logical_and(even, index == 2), couple_own)
+        when(jnp.logical_and(even, index > 1), take_parts, 2 * index - 3)
         take_side(3 * index - 1)
         relay(start + 1)
-        forward(3 * index + 2, 0)
-        when(jnp.logical_or(even, started), take_row, each(start + 1, 1))
-        when(jnp.logical_and(odd, index == 2), couple_own)
+        when(index < 3, forward, 3 * index + 2, 0)
+        when(jnp.logical_and(even, index < 3), take_row, start + 1)
+        when(jnp.logical_and(odd, index < 3), take_parts, 2 * index - 2)
+        when(ended, merge, 0, groups - 4, range(rows // 2, whole))
         when(index < 3, forward, 3 * index + 2, 1)
         relay(start + 2)
         take_side(3 * index)
-        when(start + 2 - core < whole, take_row, start + 2 - core)
+        when(index < 3, take_row, start + 2 - core)
         return carry
 
     lax.fori_loop(1, 4, main, 0)
 
-    merge_top(groups - 4, groups - 2)
+    merge(groups - 4, groups - TAIL, range(whole))
     back_copy(1 - chip).wait_recv()
     for place in range(rows - whole):
+        pair, turn = divmod(place, 2)
         for part in range(2):
             lane = slice(part * width, (part + 1) * width)
-            value = coupled[part, :, place * width : (place + 1) * width].astype(jnp.float32)
-            acc[whole + place, :, lane] = acc[whole + place, :, lane] + value
-    forward(groups - 1, 1)
-    mix_slot(near_slot, cut_of(groups - 1))
-    take_side(groups - 2)
+            value = coupled[part, pair, :, turn * width : (turn + 1) * width]
+            acc[whole + place, :, lane] = acc[whole + place, :, lane] + value.astype(jnp.float32)
+    merge(0, groups - TAIL, range(whole, rows))
+    for half in range(2):
+        forward(groups - 1, half)
+    for group in range(groups - TAIL, groups):
+        mix_slot(near_slot, cut_of(group))
 
     @pl.when(has_behind)
     def _():
-        far_copy(half_of(0), cut_of(groups - 1), groups - 1).wait_recv()
-        via_forward().wait_recv()
-
-    mix_slot(far_slot, cut_of(groups - 1))
-
-    core_copy(slice(0, whole), chan_at).wait_send()
-    core_part(chan_at).wait_send()
-    sent(lead, hs, {"chan": peer})
-    sent(rows - lead, xs, {"chan": peer})
-    sent(rows - 1, fs, {"chan": partner})
-    sent(rows, ys, {"rad": other})
+        tail_copy(every, groups - 2).wait_recv()
+
+    @pl.when(jnp.logical_and(core == 1, has_behind))
+    def _():
+        tail_copy(half_of(0), groups - 1).wait_recv()
+
+    by_core(has_behind, lambda some_rows: via_forward(some_rows).wait_recv())
+
+    def sent(owners, some_rows, sem):
+        view = xg.at[some_rows, 0 : owners * chans, :]
+        remote(view, view, sem, fl, {"chan": partner}).wait_send()
+
+    sent(peers, slice(0, rows - 1), xs)
 
     @pl.when(has_ahead)
     def _():
-        view = xg.at[0 : rows // 2, 0 : (2 * groups - 1) * GROUP, :]
-        remote(view, view, zs, zr.at[0], {"rad": ahead}).wait_send()
-        via_forward().wait_send()
-
-    @pl.when(has_behind)
-    def _():
-        via_copy().wait_send()
+        sent(1, every, zs)
+
+    by_core(has_behind, lambda some_rows: via_copy(some_rows).wait_send())
 
 
 def device_step(peers, rads, psi, k_prev, gaunt, dipole, kinetic, chan_l, field_amp):
@@ -696,61 +723,56 @@
     main_memory = pl.BlockSpec(memory_space=pltpu.HBM)
     vmem = pl.BlockSpec(memory_space=pltpu.VMEM)
     summed = jax.ShapeDtypeStruct((rows, chans, lanes), f32)
-    top = jax.ShapeDtypeStruct((2, chans, rows // 2, width), f32)
+    early = jax.ShapeDtypeStruct(psi.shape, f32)
+    far_tail = jax.ShapeDtypeStruct((rows, TAIL * GROUP, lanes), bf16)
+    mixing = jax.ShapeDtypeStruct((3, 2 * size, size), bf16)
     psi, k_prev, gaunt, dipole, kinetic, chan_l = (
         pltpu.with_memory_space_constraint(value, pltpu.HBM)
         for value in (psi, k_prev, gaunt, dipole, kinetic, chan_l.T)
     )
     parts = pl.pallas_call(
         functools.partial(fused_kernel, peers, rads),
-        out_shape=(summed, top),
+        out_shape=(summed, early, far_tail, mixing),
         in_specs=[main_memory] * 6 + [pl.BlockSpec(memory_space=pltpu.SMEM)],
-        out_specs=(vmem, vmem),
+        out_specs=(vmem,) * 4,
         scratch_shapes=[
             pltpu.VMEM(kinetic.shape, f32),
             pltpu.VMEM((2, chans), jnp.int32),
             pltpu.VMEM((2, 2, chans, rows, width), f32),
             pltpu.VMEM((rows, chans, lanes), f32),
             pltpu.VMEM((rows, peers * chans, lanes), bf16),
-            pltpu.VMEM((2, peers * chans, lanes), bf16),
-            pltpu.VMEM((2, chans, lanes), bf16),
-            pltpu.VMEM((chans, lanes), bf16),
+            pltpu.VMEM((2, PAIRS, peers * chans, lanes), bf16),
+            pltpu.VMEM((3, PAIRS, chans, lanes), bf16),
             pltpu.VMEM((2, rows, chans, lanes), bf16),
-            pltpu.VMEM((orders, chans, peers * chans), bf16),
-            pltpu.VMEM((orders, chans, peers * chans), bf16),
-            pltpu.VMEM((3, 2 * size, size), bf16),
+            pltpu.VMEM((2, orders, chans, peers * chans), bf16),
             pltpu.VMEM((lanes, lanes), bf16),
             pltpu.VMEM((chans, width), f32),
             pltpu.VMEM((chans, width), f32),
             dma((len(LOADS),)),
-            dma((4,)),
+            dma((3,)),
             dma,
             dma,
-            dma,
-            dma((rows - rows // 4,)),
-            dma,
-            dma((2,)),
+            dma((rows - rows // 4 - 2 * PAIRS + 2,)),
             dma,
             dma,
-            dma((rows - rows // 4 - 1,)),
-            dma,
+            dma((rows - rows // 4 - 2 * PAIRS + 1,)),
             dma((2, groups)),
             dma,
             dma((groups,)),
+            dma,
             dma((2,)),
-            dma((2,)),
-            pltpu.VMEM((rows // 2, GROUP, lanes), bf16),
+            pltpu.VMEM((rows, GROUP, lanes), bf16),
         ],
         compiler_params=pltpu.CompilerParams(
             collective_id=0, has_side_effects=True, vmem_limit_bytes=36 * 1024 * 1024
         ),
     )(psi, k_prev, gaunt, dipole, kinetic, chan_l, field_amp)
     return pl.pallas_call(
-        finish_kernel,
+        functools.partial(finish_kernel, rads),
         out_shape=jax.ShapeDtypeStruct(psi.shape, f32),
-        in_specs=[vmem, vmem],
+        in_specs=[vmem] * 4,
         out_specs=main_memory,
-        scratch_shapes=[pltpu.VMEM(psi.shape, f32), dma],
+        scratch_shapes=[pltpu.VMEM((2, TAIL * GROUP, rows, width), f32), dma],
         compiler_params=pltpu.CompilerParams(vmem_limit_bytes=8 * 1024 * 1024),
     )(*parts)
 

time: 43.6 us -> 42.7 us (0.979)
  Pallas kernels: 42.5 us -> 41.9 us
    pallas_call x1, Pallas kernels: 40.9 us -> 40.3 us  [device_step(): pl.pallas_call(functools.partial(fused_kernel, peers, rads), out_shape=(s...]
where the time goes in v4:
time: 42.7 us; the launch traced here: 42.6 us
  Pallas kernels  41.9 us (98%)
  between operations  0.66 us (2%)
    pallas_call x1, Pallas kernels, device_step(): pl.pallas_call(functools.partial(fused_kernel, peers, rads), out_shape=(s...  40.3 us
    pallas_call x1, Pallas kernels, device_step(): pl.pallas_call(functools.partial(finish_kernel, rads), out_shape=jax.Shap...  1.66 us

profile of v4, /device:TPU:0, one launch (start us, length us, event | category | flops | bytes accessed | tf_op | source)
XLA Modules:
  0.0 42.6 jit_solution(8904536441686376338)
XLA Ops:
  0.7 40.3 %shard_map.73 = (f32[16,192,256]{2,1,0:T(8,128)S(1)}, f32[2,192,16,128]{3,2,1,0:T(8,128)S(1)}, bf16[16,32,256]{2,1,0:T(8,128)(2,1)S(1)}, bf16[3,512,256]{2,1,0:T(8,128)(2,1)S(1)}) custom-call(f32[2,192,16,128]{3,2,1,0:T(8,128)} %psi.1, f32[2,192,16,128]{3,2,1,0:T(8,128)} %k_prev.1, bf16[4,768,768]{2,1,0:T(8,128)(2,1)} %gaunt.1, bf16[768,768]{1,0:T(8,128)(2,1)} %dipole.1, ...), custom_call_target="tpu_custom_call" | custom-call | tf_op jit(solution)/shard_map/pallas_call | solution.py:733
  40.9 1.7 %shard_map.74 = f32[2,192,16,128]{3,2,1,0:T(8,128)} custom-call(f32[16,192,256]{2,1,0:T(8,128)S(1)} %get-tuple-element.9.acc, f32[2,192,16,128]{3,2,1,0:T(8,128)S(1)} %get-tuple-element.10.early, bf16[16,32,256]{2,1,0:T(8,128)(2,1)S(1)} %get-tuple-element.11.far_tail, bf16[3,512,256]{2,1,0:T(8,128)(2,1)S(1)} %get-tuple-element.12.wr1), custom_call_target="tpu_custom_call" | custom-call | tf_op jit(solution)/shard_map/pallas_call | solution.py:770

commit v5 on v4

--- a/solution.py
+++ b/solution.py
@@ -88,12 +88,13 @@
 
 def lay_out(target, group, row, value):
     _, chans, height, width = target.shape
-    place = (pl.ds(group * GROUP * height + row, GROUP, stride=height), slice(None))
+    start = group * GROUP * height + row % height
+    place = (pl.ds(start, GROUP, stride=height), slice(None))
     target.at[0].reshape(chans * height, width)[place] = value[:, width:]
     target.at[1].reshape(chans * height, width)[place] = -value[:, :width]
 
 
-def finish_kernel(rads, acc, early, far_tail, wr1, out, late, sem):
+def finish_kernel(rads, acc, early, far_tail, wr1, out, lower, late, sem):
     rows, chans, lanes = acc.shape
     size = rows * GROUP
     done = chans - TAIL * GROUP
@@ -101,7 +102,15 @@
     minor = rad_at % 2
     behind = rad_at - 2 + 4 * minor
     has_behind = jnp.logical_and(behind >= 0, behind < rads)
-    pltpu.make_async_copy(early.at[:, 0:done], out.at[:, 0:done], sem).start()
+    half = rows // 2
+    pltpu.make_async_copy(early.at[:, 0:done], out.at[:, 0:done, 0:half, :], sem).start()
+    for first in range(0, done, 2 * GROUP):
+        for group in range(first // GROUP, first // GROUP + 2):
+            for row in range(half, rows):
+                value = acc[row, group * GROUP : (group + 1) * GROUP, :]
+                lay_out(lower, group, row, value)
+        cut = slice(first, first + 2 * GROUP)
+        pltpu.make_async_copy(lower.at[:, cut], out.at[:, cut, half:rows, :], sem).start()
 
     for group in range(TAIL):
         cut = slice(group * GROUP, (group + 1) * GROUP)
@@ -121,7 +130,7 @@
                 lay_out(late, group, row, acc[row, there, :])
 
         pltpu.make_async_copy(late.at[:, cut], out.at[:, there], sem).start()
-    pltpu.make_async_copy(early, out, sem).wait()
+    pltpu.make_async_copy(out, out, sem).wait()
 
 
 def fused_kernel(
@@ -533,7 +542,7 @@
         def _():
             relay_part(peer + 1 - 2 * core).wait_recv()
 
-        @pl.when(unit == PAIRS)
+        @pl.when(unit == 2 * PAIRS - 1)
         def _():
             back_copy(chip).start()
 
@@ -576,9 +585,9 @@
 
         lax.fori_loop(first, last, step, 0)
 
-    def merge(first, last, some_rows):
+    def merge(first, last):
         def one(group):
-            for row in some_rows:
+            for row in range(rows // 2):
                 lay_out(early, group, row, acc[row, cut_of(group), :])
 
         each_of(first, last, one)
@@ -631,7 +640,7 @@
             relay_lead(peer + 1 - 2 * core).wait_recv()
 
         when(jnp.logical_or(odd, started), take_row, each(0, start - 2))
-        when(jnp.logical_and(even, index > 1), take_parts, 2 * index - 4)
+        when(jnp.logical_and(even, index > 1), take_parts, 3 * index - 6)
         relay(start - 1)
         forward(3 * index, 1)
         take_side(3 * index - 2)
@@ -647,16 +656,16 @@
 
         take_row(start - core)
         when(started, take_side, 0)
-        when(ended, merge, 0, groups - 4, range(rows // 2))
+        when(jnp.logical_and(even, index == 2), take_parts, 1)
+        when(ended, merge, 0, groups - 4)
         forward(3 * index + 1, 1)
         when(jnp.logical_or(odd, started), take_row, each(1, start))
-        when(jnp.logical_and(even, index > 1), take_parts, 2 * index - 3)
+        when(jnp.logical_and(even, index == 2), take_parts, 2)
         take_side(3 * index - 1)
         relay(start + 1)
         when(index < 3, forward, 3 * index + 2, 0)
         when(jnp.logical_and(even, index < 3), take_row, start + 1)
         when(jnp.logical_and(odd, index < 3), take_parts, 2 * index - 2)
-        when(ended, merge, 0, groups - 4, range(rows // 2, whole))
         when(index < 3, forward, 3 * index + 2, 1)
         relay(start + 2)
         take_side(3 * index)
@@ -665,19 +674,24 @@
 
     lax.fori_loop(1, 4, main, 0)
 
-    merge(groups - 4, groups - TAIL, range(whole))
-    back_copy(1 - chip).wait_recv()
-    for place in range(rows - whole):
-        pair, turn = divmod(place, 2)
-        for part in range(2):
-            lane = slice(part * width, (part + 1) * width)
-            value = coupled[part, pair, :, turn * width : (turn + 1) * width]
-            acc[whole + place, :, lane] = acc[whole + place, :, lane] + value.astype(jnp.float32)
-    merge(0, groups - TAIL, range(whole, rows))
-    for half in range(2):
-        forward(groups - 1, half)
+    def take_back():
+        back_copy(1 - chip).wait_recv()
+        for place in range(rows - whole):
+            pair, turn = divmod(place, 2)
+            for part in range(2):
+                lane = slice(part * width, (part + 1) * width)
+                value = coupled[part, pair, :, turn * width : (turn + 1) * width]
+                acc[whole + place, :, lane] = acc[whole + place, :, lane] + value.astype(
+                    jnp.float32
+                )
+
+    merge(groups - 4, groups - TAIL)
     for group in range(groups - TAIL, groups):
+        if group == groups - 1:
+            for half in range(2):
+                forward(group, half)
         mix_slot(near_slot, cut_of(group))
+    take_back()
 
     @pl.when(has_behind)
     def _():
@@ -723,7 +737,7 @@
     main_memory = pl.BlockSpec(memory_space=pltpu.HBM)
     vmem = pl.BlockSpec(memory_space=pltpu.VMEM)
     summed = jax.ShapeDtypeStruct((rows, chans, lanes), f32)
-    early = jax.ShapeDtypeStruct(psi.shape, f32)
+    early = jax.ShapeDtypeStruct((2, chans, rows // 2, width), f32)
     far_tail = jax.ShapeDtypeStruct((rows, TAIL * GROUP, lanes), bf16)
     mixing = jax.ShapeDtypeStruct((3, 2 * size, size), bf16)
     psi, k_prev, gaunt, dipole, kinetic, chan_l = (
@@ -772,7 +786,11 @@
         out_shape=jax.ShapeDtypeStruct(psi.shape, f32),
         in_specs=[vmem] * 4,
         out_specs=main_memory,
-        scratch_shapes=[pltpu.VMEM((2, TAIL * GROUP, rows, width), f32), dma],
+        scratch_shapes=[
+            pltpu.VMEM((2, chans - TAIL * GROUP, rows // 2, width), f32),
+            pltpu.VMEM((2, TAIL * GROUP, rows, width), f32),
+            dma,
+        ],
         compiler_params=pltpu.CompilerParams(vmem_limit_bytes=8 * 1024 * 1024),
     )(*parts)
 

time: 42.7 us -> 42.6 us (level)
  no operation moved by 1% of the time
where the time goes in v5:
time: 42.6 us; the launch traced here: 42.4 us
  Pallas kernels  41.7 us (98%)
  between operations  0.66 us (2%)
    pallas_call x1, Pallas kernels, device_step(): pl.pallas_call(functools.partial(fused_kernel, peers, rads), out_shape=(s...  40.1 us
    pallas_call x1, Pallas kernels, device_step(): pl.pallas_call(functools.partial(finish_kernel, rads), out_shape=jax.Shap...  1.67 us

profile of v5, /device:TPU:0, one launch (start us, length us, event | category | flops | bytes accessed | tf_op | source)
XLA Modules:
  0.0 42.4 jit_solution(6038387325563818216)
XLA Ops:
  0.7 40.1 %shard_map.73 = (f32[16,192,256]{2,1,0:T(8,128)S(1)}, f32[2,192,8,128]{3,2,1,0:T(8,128)S(1)}, bf16[16,32,256]{2,1,0:T(8,128)(2,1)S(1)}, bf16[3,512,256]{2,1,0:T(8,128)(2,1)S(1)}) custom-call(f32[2,192,16,128]{3,2,1,0:T(8,128)} %psi.1, f32[2,192,16,128]{3,2,1,0:T(8,128)} %k_prev.1, bf16[4,768,768]{2,1,0:T(8,128)(2,1)} %gaunt.1, bf16[768,768]{1,0:T(8,128)(2,1)} %dipole.1, ...), custom_call_target="tpu_custom_call" | custom-call | tf_op jit(solution)/shard_map/pallas_call | solution.py:747
  40.7 1.7 %shard_map.74 = f32[2,192,16,128]{3,2,1,0:T(8,128)} custom-call(f32[16,192,256]{2,1,0:T(8,128)S(1)} %get-tuple-element.9.acc, f32[2,192,8,128]{3,2,1,0:T(8,128)S(1)} %get-tuple-element.10.early, bf16[16,32,256]{2,1,0:T(8,128)(2,1)S(1)} %get-tuple-element.11.far_tail, bf16[3,512,256]{2,1,0:T(8,128)(2,1)S(1)} %get-tuple-element.12.wr1), custom_call_target="tpu_custom_call" | custom-call | tf_op jit(solution)/shard_map/pallas_call | solution.py:784

commit v6 on v5

--- a/solution.py
+++ b/solution.py
@@ -78,7 +78,7 @@
 GROUP = 16
 PAIRS = 2
 TAIL = 2
-LOADS = ((0, 1), (1, 4), (4, 12))
+LOADS = ((0, 1), (1, 3), (3, 6), (6, 9), (9, 12))
 
 
 def split_bf16(value):
@@ -318,10 +318,6 @@
         pltpu.make_async_copy(kin_main, kin, small_sem.at[0]),
         pltpu.make_async_copy(chan_main, chan_l, small_sem.at[1]),
     ]
-    for part in range(len(LOADS)):
-        for which in range(2):
-            load(which, part).start()
-
     barrier = pltpu.get_barrier_semaphore()
     for step in range(1, chips):
         pl.semaphore_signal(
@@ -337,6 +333,10 @@
     @pl.when(has_behind)
     def _():
         pl.semaphore_signal(barrier, inc=1, device_id={"rad": behind}, device_id_type=MESH)
+
+    for part in range(len(LOADS)):
+        for which in range(2):
+            load(which, part).start()
 
     def form(group):
         for part in range(2):
@@ -441,6 +441,10 @@
                 jnp.bfloat16
             )
 
+    @pl.when(core == 0)
+    def _():
+        pass_on(0, 0)
+
     @pl.when(core == 1)
     def _():
         pass_on(0, 1)
@@ -598,7 +602,10 @@
             lead_copy(block(peer)).wait_recv()
             relay_lead(peer).start()
 
-    forward(0, 0)
+    @pl.when(core == 1)
+    def _():
+        pass_on(1, 0)
+
     each_of(0, 3, own_group)
     forward(0, 1)
     each_of(3, 4, own_group)

time: 42.6 us -> 42.6 us (level)
  no operation moved by 1% of the time
where the time goes in v6:
time: 42.6 us; the launch traced here: 42.4 us
  Pallas kernels  41.7 us (98%)
  between operations  0.66 us (2%)
    pallas_call x1, Pallas kernels, device_step(): pl.pallas_call(functools.partial(fused_kernel, peers, rads), out_shape=(s...  40.1 us
    pallas_call x1, Pallas kernels, device_step(): pl.pallas_call(functools.partial(finish_kernel, rads), out_shape=jax.Shap...  1.67 us

profile of v6, /device:TPU:0, one launch (start us, length us, event | category | flops | bytes accessed | tf_op | source)
XLA Modules:
  0.0 42.4 jit_solution(6166046928956159257)
XLA Ops:
  0.7 40.1 %shard_map.73 = (f32[16,192,256]{2,1,0:T(8,128)S(1)}, f32[2,192,8,128]{3,2,1,0:T(8,128)S(1)}, bf16[16,32,256]{2,1,0:T(8,128)(2,1)S(1)}, bf16[3,512,256]{2,1,0:T(8,128)(2,1)S(1)}) custom-call(f32[2,192,16,128]{3,2,1,0:T(8,128)} %psi.1, f32[2,192,16,128]{3,2,1,0:T(8,128)} %k_prev.1, bf16[4,768,768]{2,1,0:T(8,128)(2,1)} %gaunt.1, bf16[768,768]{1,0:T(8,128)(2,1)} %dipole.1, ...), custom_call_target="tpu_custom_call" | custom-call | tf_op jit(solution)/shard_map/pallas_call | solution.py:754
  40.7 1.7 %shard_map.74 = f32[2,192,16,128]{3,2,1,0:T(8,128)} custom-call(f32[16,192,256]{2,1,0:T(8,128)S(1)} %get-tuple-element.9.acc, f32[2,192,8,128]{3,2,1,0:T(8,128)S(1)} %get-tuple-element.10.early, bf16[16,32,256]{2,1,0:T(8,128)(2,1)S(1)} %get-tuple-element.11.far_tail, bf16[3,512,256]{2,1,0:T(8,128)(2,1)S(1)} %get-tuple-element.12.wr1), custom_call_target="tpu_custom_call" | custom-call | tf_op jit(solution)/shard_map/pallas_call | solution.py:791

commit v7 on v6

--- a/solution.py
+++ b/solution.py
@@ -357,14 +357,23 @@
     def send_group(group):
         for half in range(2):
             side_copy(group, half).start()
-        lead_copy(block_cut(chan_at, group)).start()
+        alone = jnp.logical_or(group == 0, group == groups - 1)
+
+        @pl.when(alone)
+        def _():
+            lead_copy(block_cut(chan_at, group)).start()
+
+        @pl.when(jnp.logical_and(jnp.logical_not(alone), group % 2 == 0))
+        def _():
+            start = pl.multiple_of(chan_at * chans + (group - 1) * GROUP, GROUP)
+            lead_copy(pl.ds(start, 2 * GROUP)).start()
 
     arrive(0)
     form(jnp.int32(0))
     pl.semaphore_wait(
         barrier, chips + 1 + has_ahead.astype(jnp.int32) + has_behind.astype(jnp.int32)
     )
-    send_group(0)
+    send_group(jnp.int32(0))
     arrive(1)
     form(jnp.int32(1))
 
@@ -383,7 +392,7 @@
         for kind in range(2):
             load_weight(kind, order).start()
 
-    send_group(groups - 1)
+    send_group(jnp.int32(groups - 1))
 
     by_core(has_behind, lambda some_rows: via_copy(some_rows).start())
 

time: 42.6 us -> 42.7 us (level)
  no operation moved by 1% of the time
where the time goes in v7:
time: 42.7 us; the launch traced here: 42.4 us
  Pallas kernels  41.7 us (98%)
  between operations  0.66 us (2%)
    pallas_call x1, Pallas kernels, device_step(): pl.pallas_call(functools.partial(fused_kernel, peers, rads), out_shape=(s...  40.1 us
    pallas_call x1, Pallas kernels, device_step(): pl.pallas_call(functools.partial(finish_kernel, rads), out_shape=jax.Shap...  1.67 us

profile of v7, /device:TPU:0, one launch (start us, length us, event | category | flops | bytes accessed | tf_op | source)
XLA Modules:
  0.0 42.4 jit_solution(2619786381422790649)
XLA Ops:
  0.7 40.1 %shard_map.73 = (f32[16,192,256]{2,1,0:T(8,128)S(1)}, f32[2,192,8,128]{3,2,1,0:T(8,128)S(1)}, bf16[16,32,256]{2,1,0:T(8,128)(2,1)S(1)}, bf16[3,512,256]{2,1,0:T(8,128)(2,1)S(1)}) custom-call(f32[2,192,16,128]{3,2,1,0:T(8,128)} %psi.1, f32[2,192,16,128]{3,2,1,0:T(8,128)} %k_prev.1, bf16[4,768,768]{2,1,0:T(8,128)(2,1)} %gaunt.1, bf16[768,768]{1,0:T(8,128)(2,1)} %dipole.1, ...), custom_call_target="tpu_custom_call" | custom-call | tf_op jit(solution)/shard_map/pallas_call | solution.py:763
  40.7 1.7 %shard_map.74 = f32[2,192,16,128]{3,2,1,0:T(8,128)} custom-call(f32[16,192,256]{2,1,0:T(8,128)S(1)} %get-tuple-element.9.acc, f32[2,192,8,128]{3,2,1,0:T(8,128)S(1)} %get-tuple-element.10.early, bf16[16,32,256]{2,1,0:T(8,128)(2,1)S(1)} %get-tuple-element.11.far_tail, bf16[3,512,256]{2,1,0:T(8,128)(2,1)S(1)} %get-tuple-element.12.wr1), custom_call_target="tpu_custom_call" | custom-call | tf_op jit(solution)/shard_map/pallas_call | solution.py:800
